TPU v7x, 32 devices: a whole 2x2x4 slice. The times are simulated.
32 devices in a mesh: energy: 2 (over x), mom: 16 (over z, y, core).
Axes of the slice: x: 2, y: 2, z: 4, core: 2. Of those that a mesh axis runs over, the one named last changes fastest.
Arguments:
- source: float32 [256, 128, 1024], P(('energy', 'mom')), parts along dimension 0, may hold values from -6 to 6
- green: float32 [256, 1024], P(('energy', 'mom')), parts along dimension 0, may hold values from 0.1 to 0.6
- couple_one: float32 [2, 4, 128, 128], replicated, may hold values from -0.5 to 0.5
- couple_two: float32 [2, 4, 128, 128], replicated, may hold values from -0.5 to 0.5
- p_bracket: int32 [2, 1024], replicated, may hold values from 0 to 28
- q_bracket: int32 [2, 1024], replicated, may hold values from 0 to 28
- p_weight: float32 [2, 4, 1024], replicated, may hold values from -0.25 to 1
- q_weight: float32 [2, 4, 1024], replicated, may hold values from -0.25 to 1
- qr_bracket: int32 [2, 1024], replicated, may hold values from 0 to 28
- r_bracket: int32 [2, 1024], replicated, may hold values from 0 to 28
- qr_weight: float32 [2, 4, 1024], replicated, may hold values from -0.25 to 1
- r_weight: float32 [2, 4, 1024], replicated, may hold values from -0.25 to 1
Outputs:
- amplitude: float32 [256, 128, 1024], P(('energy', 'mom')), parts along dimension 0
- component: float32 [256, 128, 1024], P(('energy', 'mom')), parts along dimension 0
There are 2 independent parts, one for each index of `energy`. A program takes and returns all parts, laid end to end along the dimension named above; an argument that names none is the same for every part. Nothing has to cross between parts.
All inputs are finite; a program needn't handle non-finite values.
Results may differ from a plain program's by a relative error of at most 0.0001.
Values sent between devices are 32-bit elements; how exact they have to be, the bound alone decides.
No kernel may reach another device: no remote copies, remote signals or barrier semaphores. Data moves between devices by JAX's collectives and lax.ppermute only.
A program may use at most 128 MiB of HBM per device.

v0:
```python
import functools


import jax
import jax.numpy as jnp
from jax import lax
from jax.experimental import pallas as pl
from jax.experimental.pallas import tpu as pltpu
from jax.sharding import PartitionSpec as P

ITERS = 2
LANES = 128
F32 = jnp.float32
BF16 = jnp.bfloat16
VMEM_LIMIT = 60 << 20
PIECES = 4
TILES = 4
SOURCE_ROWS = 4


def split(value):
    high = value.astype(BF16)
    return high, (value - high.astype(F32)).astype(BF16)


def dot(a, b):
    return jnp.dot(a, b, preferred_element_type=F32)


def dot_nt(a, b):
    return lax.dot_general(a, b, (((1,), (1,)), ((), ())), preferred_element_type=F32)


def call(kernel, flops, moved, args, grid, in_specs, out_specs, out_shape, scratch_shapes=(), scalars=(), aliases=None):
    return pl.pallas_call(
        kernel,
        grid_spec=pltpu.PrefetchScalarGridSpec(
            num_scalar_prefetch=len(scalars),
            grid=grid,
            in_specs=in_specs,
            out_specs=out_specs,
            scratch_shapes=scratch_shapes,
        ),
        out_shape=out_shape,
        input_output_aliases=aliases or {},
        compiler_params=pltpu.CompilerParams(vmem_limit_bytes=VMEM_LIMIT),
        cost_estimate=pl.CostEstimate(flops=flops, bytes_accessed=moved, transcendentals=0),
    )(*scalars, *args)


def map_factors(count, k, rows, first_ref, second_ref, first_weight_ref, second_weight_ref):
    size = rows.size
    table = jnp.concatenate(
        [
            first_ref[k : k + 1, rows].astype(F32),
            second_ref[k : k + 1, rows].astype(F32),
            first_weight_ref[k, :, rows],
            second_weight_ref[k, :, rows],
            jnp.zeros((6, size), F32),
        ],
        axis=0,
    ).T
    lane = lax.broadcasted_iota(jnp.int32, (1, LANES), 1)

    def factor(index, base):
        grid = index.astype(F32) - table[:, base : base + 1]
        total = jnp.zeros((size, LANES), F32)
        for offset in range(4):
            column = 2 + 4 * base + offset
            total = jnp.where(grid == offset, table[:, column : column + 1], total)
        return total

    high, low = split(factor(lane, 0))
    return high, low, factor(lane - lax.div(lane, count) * count, 1)


def chosen_nodes(count, columns):
    node = lax.broadcasted_iota(jnp.int32, (LANES, columns), 0)
    column = lax.broadcasted_iota(jnp.int32, (LANES, columns), 1)
    inside = jnp.logical_and(column >= node * count, column < (node + 1) * count)
    return jnp.where(inside, 1.0, 0.0).astype(BF16)


def build_rows(count, rows, inputs, chosen, high_ref, low_ref):
    angles, size = inputs[0].shape
    for k in range(angles):
        first_high, first_low, second = map_factors(count, k, rows, *inputs)
        for tile in range(size // LANES):
            lanes = slice(tile * LANES, (tile + 1) * LANES)
            spread = dot(first_high, chosen[:, lanes]) + dot(first_low, chosen[:, lanes])
            high, low = split(spread * second)
            lanes = slice(k * size + tile * LANES, k * size + (tile + 1) * LANES)
            high_ref[:, lanes] = high
            low_ref[:, lanes] = low


def map_kernel(count, *refs):
    inputs, (high_ref, low_ref) = refs[:4], refs[4:]
    size = high_ref.shape[0]
    start = pl.multiple_of(pl.program_id(0) * size, size)
    chosen = chosen_nodes(count, inputs[0].shape[1])
    build_rows(count, pl.ds(start, size), inputs, chosen, high_ref, low_ref)


def spline_maps(first, second, first_weight, second_weight, count):
    angles, size = first.shape
    tile = size // PIECES
    out = jax.ShapeDtypeStruct((size, angles * size), BF16)
    spec = pl.BlockSpec((tile, angles * size), lambda i: (i, 0))
    return call(
        functools.partial(map_kernel, count),
        10 * angles * size * size,
        4 * angles * size * size,
        (first, second, first_weight, second_weight),
        grid=(PIECES,),
        in_specs=[pl.BlockSpec(memory_space=pltpu.VMEM)] * 4,
        out_specs=[spec, spec],
        out_shape=[out, out],
    )


def interpolate(high_ref, low_ref, mixed_high, mixed_low, product):
    high = high_ref[...]
    return (
        product(high, mixed_high[...])
        + product(high, mixed_low[...])
        + product(low_ref[...], mixed_high[...])
    )


def spread_out(flip, value, out_ref, scale_ref=None):
    parts, blocks, near, local, count, channels = out_ref.shape
    rows = near * count
    for b in range(blocks):
        for n in range(local):
            at = b * local + n
            block = value[:, at * channels : (at + 1) * channels]
            if scale_ref is not None:
                block = block * scale_ref[:, at : at + 1]
            for j in range(parts):
                piece = block[j * rows : (j + 1) * rows].reshape(near, count, channels)
                out_ref[j ^ (flip & (parts - 1)), b, :, n, :, :] = piece


def out_spec(shape, tile):
    parts = shape[0] // TILES
    return pl.BlockSpec(
        (parts,) + shape[1:],
        lambda i, flip: (tile(i) ^ lax.div(flip[0], parts), 0, 0, 0, 0, 0),
    )


def gather(me, sets, whole_ref):
    blocks, local, _, _ = whole_ref.shape
    per = sets[0][0].shape[3]
    for s in range(len(sets[0])):
        rows = pl.ds(pl.multiple_of((me ^ s) * per, per), per)
        for b in range(blocks):
            for n in range(local):
                value = sets[0][s][0, b, n]
                for other in sets[1:]:
                    value = value + other[s][0, b, n]
                whole_ref[b, n, rows, :] = value


def finish_rows(flip, t, value, held_ref, out_ref, sems, scale_ref=None):
    devices, blocks, near, local, count, channels = held_ref.shape
    parts = devices // PIECES
    rows = near * count
    group = t ^ lax.div(flip, parts)
    for b in range(blocks):
        for n in range(local):
            at = b * local + n
            block = value[:, at * channels : (at + 1) * channels]
            if scale_ref is not None:
                start = pl.multiple_of(t * parts * rows, parts * rows)
                block = block * scale_ref[pl.ds(start, parts * rows), at : at + 1]
            for j in range(parts):
                piece = block[j * rows : (j + 1) * rows].reshape(near, count, channels)
                held_ref[group * parts + (j ^ (flip & (parts - 1))), b, :, n, :, :] = piece
    part = pl.ds(group * parts, parts)
    pltpu.make_async_copy(held_ref.at[part], out_ref.at[part], sems.at[group]).start()


def finish_copies(held_ref, out_ref, sems):
    parts = held_ref.shape[0] // PIECES
    for t in range(PIECES):
        part = pl.ds(t * parts, parts)
        pltpu.make_async_copy(held_ref.at[part], out_ref.at[part], sems.at[t]).wait()


def mix_source(blocks, source_ref, held, sems, couple_ref, m_high, m_low):
    angles, _, channels, _ = couple_ref.shape
    rows, _, size = held.shape
    quarter = channels // 4
    count = angles * len(blocks) * quarter
    local = rows // 4

    def step(row, carry):
        pltpu.make_async_copy(source_ref.at[row], held.at[row], sems.at[row]).wait()
        r, c = lax.div(row, 4), lax.rem(row, 4)
        picked = [
            couple_ref[k, c, g * quarter : (g + 1) * quarter, :]
            for k in range(angles)
            for g in blocks
        ]
        w_high, w_low = split(jnp.concatenate(picked, axis=0))
        high, low = split(held[row])
        both = dot(jnp.concatenate([w_high, w_low], axis=0), high)
        high, low = split(both[:count] + both[count:] + dot(w_high, low))
        for k in range(angles):
            lanes = slice(k * size, (k + 1) * size)
            for b in range(len(blocks)):
                at = (k * len(blocks) + b) * quarter
                to = pl.multiple_of((b * local + r) * channels + c * quarter, quarter)
                m_high[pl.ds(to, quarter), lanes] = high[at : at + quarter]
                m_low[pl.ds(to, quarter), lanes] = low[at : at + quarter]
        return carry

    lax.fori_loop(0, rows, step, 0)


def building_kernel(blocks, count, flip_ref, source_ref, couple_ref, *refs):
    inputs = refs[:4]
    out_ref, made_high, made_low = refs[4:7]
    held_source, source_sems, high_buf, low_buf, map_sems, m_high, m_low, held_ref, sems = refs[7:]
    for row in range(source_ref.shape[0]):
        pltpu.make_async_copy(source_ref.at[row], held_source.at[row], source_sems.at[row]).start()
    mix_source(blocks, source_ref, held_source, source_sems, couple_ref, m_high, m_low)
    size = inputs[0].shape[1]
    rows = size // PIECES
    chosen = chosen_nodes(count, size)
    made = ((high_buf, made_high), (low_buf, made_low))

    def step(t, carry):
        part = pl.ds(pl.multiple_of(t * rows, rows), rows)
        build_rows(count, part, inputs, chosen, high_buf.at[part], low_buf.at[part])
        for n, (buf, to) in enumerate(made):
            pltpu.make_async_copy(buf.at[part], to.at[part], map_sems.at[n, t]).start()
        value = interpolate(high_buf.at[part], low_buf.at[part], m_high, m_low, dot_nt)
        finish_rows(flip_ref[0], t, value, held_ref, out_ref, sems)
        return carry

    lax.fori_loop(0, PIECES, step, 0)
    finish_copies(held_ref, out_ref, sems)
    for t in range(PIECES):
        part = pl.ds(t * rows, rows)
        for n, (buf, to) in enumerate(made):
            pltpu.make_async_copy(buf.at[part], to.at[part], map_sems.at[n, t]).wait()


def first_one_building(blocks, flip, source, couple, inputs, near, devices, count):
    rows, channels, size = source.shape
    local = rows // 4
    angles = couple.shape[0]
    out = (devices, len(blocks), near, local, size // (devices * near), channels)
    wide = len(blocks) * local * channels
    vmem = pl.BlockSpec(memory_space=pltpu.VMEM)
    anywhere = pl.BlockSpec(memory_space=pl.ANY)
    made = jax.ShapeDtypeStruct((size, angles * size), BF16)
    return call(
        functools.partial(building_kernel, blocks, count),
        6 * wide * angles * size * (size + channels),
        4 * source.size + 4 * angles * size * size,
        (source, couple, *inputs),
        grid=(),
        in_specs=[anywhere] + [vmem] * 5,
        out_specs=[anywhere] * 3,
        out_shape=[jax.ShapeDtypeStruct(out, F32), made, made],
        scratch_shapes=[pltpu.VMEM(source.shape, F32), pltpu.SemaphoreType.DMA((rows,))]
        + [pltpu.VMEM(made.shape, BF16)] * 2
        + [pltpu.SemaphoreType.DMA((2, PIECES))]
        + [pltpu.VMEM((wide, angles * size), BF16)] * 2
        + [pltpu.VMEM(out, F32), pltpu.SemaphoreType.DMA((PIECES,))],
        scalars=(flip,),
    )


def first_kernel(blocks, steps, flip_ref, source_ref, couple_ref, high_ref, low_ref, out_ref, m_high, m_low):
    angles, _, channels, _ = couple_ref.shape
    quarter = channels // 4
    together, _, size = source_ref.shape
    i = pl.program_id(0)
    count = angles * len(blocks) * quarter
    local = steps * together // 4

    @pl.when(i < steps)
    def _():
        for n in range(together):
            row = i * together + n
            r, c = lax.div(row, 4), lax.rem(row, 4)
            rows = [
                couple_ref[k, c, g * quarter : (g + 1) * quarter, :]
                for k in range(angles)
                for g in blocks
            ]
            w_high, w_low = split(jnp.concatenate(rows, axis=0))
            high, low = split(source_ref[n])
            both = dot(jnp.concatenate([w_high, w_low], axis=0), high)
            high, low = split(both[:count] + both[count:] + dot(w_high, low))
            for k in range(angles):
                lanes = slice(k * size, (k + 1) * size)
                for b in range(len(blocks)):
                    at = (k * len(blocks) + b) * quarter
                    to = pl.multiple_of((b * local + r) * channels + c * quarter, quarter)
                    m_high[pl.ds(to, quarter), lanes] = high[at : at + quarter]
                    m_low[pl.ds(to, quarter), lanes] = low[at : at + quarter]

    @pl.when(i >= steps)
    def _():
        spread_out(flip_ref[0], interpolate(high_ref, low_ref, m_high, m_low, dot_nt), out_ref)


def first_one(blocks, flip, source, couple, maps, near, devices):
    rows, channels, size = source.shape
    local = rows // 4
    angles = couple.shape[0]
    together = SOURCE_ROWS
    steps = rows // together
    out = (devices, len(blocks), near, local, size // (devices * near), channels)
    wide = len(blocks) * local * channels

    def tile(i):
        return jnp.maximum(i - steps, 0)

    return call(
        functools.partial(first_kernel, blocks, steps),
        6 * wide * angles * size * (size + channels),
        4 * source.size + 4 * angles * size * size,
        (source, couple, *maps),
        grid=(steps + TILES,),
        in_specs=[
            pl.BlockSpec((together, channels, size), lambda i, f: (jnp.minimum(i, steps - 1), 0, 0)),
            pl.BlockSpec(couple.shape, lambda i, f: (0, 0, 0, 0)),
        ]
        + [pl.BlockSpec((size // TILES, angles * size), lambda i, f: (tile(i), 0))] * 2,
        out_specs=out_spec(out, tile),
        out_shape=jax.ShapeDtypeStruct(out, F32),
        scratch_shapes=[pltpu.VMEM((wide, angles * size), BF16)] * 2,
        scalars=(flip,),
    )


def chunk_specs(chunk):
    if not isinstance(chunk, list):
        return [chunk], [pl.BlockSpec(chunk.shape, lambda i, f: (0, 0, 0, 0, 0))]
    spec = pl.BlockSpec((1,) + chunk[0].shape[1:], lambda i, f: (0, 0, 0, 0, 0))
    return chunk, [spec] * len(chunk)


def later_kernel(blocks, counts, flip_ref, *refs):
    chunks = []
    for count in counts:
        chunks.append(refs[:count])
        refs = refs[count:]
    couple_ref, high_ref, low_ref, out_ref, w_high, w_low, m_high, m_low = refs[:8]
    wholes = list(refs[8:])
    angles, _, channels, _ = couple_ref.shape
    quarter = channels // 4
    size = high_ref.shape[1] // angles
    _, _, local, per, _ = chunks[0][0].shape

    @pl.when(pl.program_id(0) == 0)
    def _():
        lane = lax.broadcasted_iota(jnp.int32, (quarter, channels), 1)
        for k in range(angles):
            for b, g in enumerate(blocks):
                for c in range(4):
                    rows = couple_ref[k, c, g * quarter : (g + 1) * quarter, :]
                    at = (k * len(blocks) + b) * channels + c * quarter
                    inside = lax.div(lane, quarter) == c
                    for other in range(4):
                        shift = ((c - other) * quarter) % channels
                        moved = pltpu.roll(rows, shift, 1) if shift else rows
                        high, low = split(jnp.where(inside, moved, 0.0))
                        lanes = slice(other * channels, (other + 1) * channels)
                        w_high[at : at + quarter, lanes] = high
                        w_low[at : at + quarter, lanes] = low
        sources = []
        for chunk in chunks:
            if len(chunk) > 1:
                whole = wholes.pop(0)
                gather(flip_ref[1], [chunk], whole)
                sources += [(whole, b, True) for b in range(whole.shape[0])]
            else:
                sources += [(chunk[0], b, False) for b in range(chunk[0].shape[1])]
        rows = min(256, size)

        def step(t, carry):
            for r in range(local):
                pieces = []
                for ref, b, flat in sources:
                    if flat:
                        pieces.append(ref[b, r, pl.ds(pl.multiple_of(t * rows, rows), rows), :])
                    else:
                        piece = ref[pl.ds(t * (rows // per), rows // per), b, r]
                        pieces.append(piece.reshape(rows, channels))
                high, low = split(jnp.concatenate(pieces, axis=1))
                mixed = (
                    dot_nt(high, w_high[...]) + dot_nt(low, w_high[...]) + dot_nt(high, w_low[...])
                )
                high, low = split(mixed)
                for k in range(angles):
                    here = pl.ds(pl.multiple_of(k * size + t * rows, rows), rows)
                    for b in range(len(blocks)):
                        at = (k * len(blocks) + b) * channels
                        to = (b * local + r) * channels
                        m_high[here, to : to + channels] = high[:, at : at + channels]
                        m_low[here, to : to + channels] = low[:, at : at + channels]
            return carry

        lax.fori_loop(0, size // rows, step, 0)

    spread_out(flip_ref[0], interpolate(high_ref, low_ref, m_high, m_low, dot), out_ref)


def later_one(blocks, flip, chunks, couple, maps, near, devices):
    _, _, local, per, channels = chunks[0][0].shape if isinstance(chunks[0], list) else chunks[0].shape
    size = devices * per
    angles = couple.shape[0]
    out = (devices, len(blocks), near, local, size // (devices * near), channels)
    wide = len(blocks) * local * channels
    operands, specs, counts, wholes = [], [], [], []
    for chunk in chunks:
        some, some_specs = chunk_specs(chunk)
        operands += some
        specs += some_specs
        counts.append(len(some))
        if isinstance(chunk, list):
            wholes.append(pltpu.VMEM((chunk[0].shape[1], local, size, channels), F32))
    return call(
        functools.partial(later_kernel, blocks, counts),
        6 * wide * angles * size * (size + 4 * channels),
        16 * local * size * channels + 4 * angles * size * size,
        (*operands, couple, *maps),
        grid=(TILES,),
        in_specs=specs
        + [pl.BlockSpec(couple.shape, lambda i, f: (0, 0, 0, 0))]
        + [pl.BlockSpec((size // TILES, angles * size), lambda i, f: (i, 0))] * 2,
        out_specs=out_spec(out, lambda i: i),
        out_shape=jax.ShapeDtypeStruct(out, F32),
        scratch_shapes=[pltpu.VMEM((angles * len(blocks) * channels, 4 * channels), BF16)] * 2
        + [pltpu.VMEM((angles * size, wide), BF16)] * 2
        + wholes,
        scalars=(flip,),
    )


def two_kernel(blocks, counts, flip_ref, *refs):
    chunks = []
    for count in counts:
        chunks.append(refs[:count])
        refs = refs[count:]
    couple_ref, green_ref, high_ref, low_ref, out_ref, turned, w_high, w_low, m_high, m_low = refs[:10]
    angles, _, channels, _ = couple_ref.shape
    quarter = channels // 4
    size = high_ref.shape[1] // angles
    _, _, local, per, _ = chunks[0][0].shape

    @pl.when(pl.program_id(0) == 0)
    def _():
        for k in range(angles):
            for b, g in enumerate(blocks):
                at = k * len(blocks) + b
                rows = [couple_ref[k, g, pl.ds(c, quarter, stride=4), :] for c in range(4)]
                turned[at] = jnp.concatenate(rows, axis=0).T
                rows = [turned[at, pl.ds(c, quarter, stride=4), :] for c in range(4)]
                high, low = split(jnp.concatenate(rows, axis=0))
                w_high[b, :, k * channels : (k + 1) * channels] = high
                w_low[b, :, k * channels : (k + 1) * channels] = low
        if counts[0] > 1:
            gather(flip_ref[1], chunks, refs[10])
        rows = min(256, size)

        def step(t, carry):
            for b in range(len(blocks)):
                for p in range(local):
                    if counts[0] > 1:
                        here = pl.ds(pl.multiple_of(t * rows, rows), rows)
                        value = refs[10][b, p, here, :]
                    else:
                        here = pl.ds(t * (rows // per), rows // per)
                        value = chunks[0][0][here, b, p]
                        for other in chunks[1:]:
                            value = value + other[0][here, b, p]
                        value = value.reshape(rows, channels)
                    high, low = split(value)
                    mixed = dot(high, w_high[b]) + dot(low, w_high[b]) + dot(high, w_low[b])
                    high, low = split(mixed)
                    to = (b * local + p) * channels
                    for k in range(angles):
                        here = pl.ds(pl.multiple_of(k * size + t * rows, rows), rows)
                        lanes = slice(k * channels, (k + 1) * channels)
                        m_high[here, to : to + channels] = high[:, lanes]
                        m_low[here, to : to + channels] = low[:, lanes]
            return carry

        lax.fori_loop(0, size // rows, step, 0)

    spread_out(flip_ref[0], interpolate(high_ref, low_ref, m_high, m_low, dot), out_ref, green_ref)


def component_two(blocks, flip, chunks, couple, green, maps, near, devices):
    _, _, local, per, channels = chunks[0][0].shape if isinstance(chunks[0], list) else chunks[0].shape
    size = devices * per
    angles = couple.shape[0]
    out = (devices, len(blocks), near, local, per // near, channels)
    wide = len(blocks) * local * channels
    operands, specs, counts = [], [], []
    for chunk in chunks:
        some, some_specs = chunk_specs(chunk)
        operands += some
        specs += some_specs
        counts.append(len(some))
    wholes = [pltpu.VMEM((len(blocks), local, size, channels), F32)] if counts[0] > 1 else []
    return call(
        functools.partial(two_kernel, blocks, counts),
        6 * wide * angles * size * (size + channels),
        4 * len(chunks) * wide * size + 4 * angles * size * size,
        (*operands, couple, green, *maps),
        grid=(TILES,),
        in_specs=specs
        + [
            pl.BlockSpec(couple.shape, lambda i, f: (0, 0, 0, 0)),
            pl.BlockSpec((size // TILES, green.shape[1]), lambda i, f: (i, 0)),
        ]
        + [pl.BlockSpec((size // TILES, angles * size), lambda i, f: (i, 0))] * 2,
        out_specs=out_spec(out, lambda i: i),
        out_shape=jax.ShapeDtypeStruct(out, F32),
        scratch_shapes=[pltpu.VMEM((angles * len(blocks), channels, channels), F32)]
        + [pltpu.VMEM((len(blocks), channels, angles * channels), BF16)] * 2
        + [pltpu.VMEM((angles * size, wide), BF16)] * 2
        + wholes,
        scalars=(flip,),
    )


def amplitude_kernel(quarter, count, flip_ref, source_ref, *refs):
    backs, out_ref = refs[:count], refs[-1]
    if count > 1:
        out_ref, whole_ref = refs[-2:]
        per = backs[0].shape[1]
        for s in range(count):
            rows = pl.ds(pl.multiple_of((flip_ref[1] ^ s) * per, per), per)
            whole_ref[rows, :] = backs[s][0]
        turned = whole_ref[...].T
    else:
        back = backs[0][...]
        turned = back.reshape(-1, back.shape[-1]).T
    for c in range(4):
        out_ref[c] = source_ref[c] + turned[c * quarter : (c + 1) * quarter]


def amplitude_chunk(blocks, flip, source, chunk, so_far):
    _, channels, size = source.shape
    quarter = channels // 4
    backs = chunk if isinstance(chunk, list) else [chunk]
    _, _, local, per, _ = backs[0].shape
    spec = pl.BlockSpec((4, quarter, size), lambda b, r, f: (r, blocks[0] + b, 0))
    depth = 1 if len(backs) > 1 else backs[0].shape[0]
    back_spec = pl.BlockSpec((depth, None, None, per, channels), lambda b, r, f: (0, b, r, 0, 0))
    in_specs = [spec] + [back_spec] * len(backs)
    args = [source, *backs]
    aliases = {}
    if so_far is not None:
        in_specs.append(pl.BlockSpec(memory_space=pl.ANY))
        args.append(so_far)
        aliases = {len(args): 0}
    moved = len(blocks) * local * channels * size
    return call(
        functools.partial(amplitude_kernel, quarter, len(backs)),
        moved,
        12 * moved,
        args,
        grid=(len(blocks), local),
        in_specs=in_specs,
        out_specs=spec,
        out_shape=jax.ShapeDtypeStruct(source.shape, F32),
        scratch_shapes=[pltpu.VMEM((size, channels), F32)] if len(backs) > 1 else [],
        scalars=(flip,),
        aliases=aliases,
    )


def output_kernel(quarter, flip_ref, sent_ref, *refs):
    out_ref, whole_ref, turned_ref = refs[-3:]
    devices, near, count, channels = sent_ref.shape
    per_tile = LANES // (devices * near)
    for d in range(devices):
        whole_ref[d] = sent_ref[d ^ flip_ref[0]]
    for tile in range(count // per_tile):
        rows = [
            whole_ref[:, :, tile * per_tile + i, :].reshape(devices * near, channels)
            for i in range(per_tile)
        ]
        turned = jnp.concatenate(rows, axis=0).T
        for c in range(4):
            turned_ref[tile, pl.ds(c, quarter, stride=4), :] = turned[
                c * quarter : (c + 1) * quarter
            ]
        out_ref[:, tile * LANES : (tile + 1) * LANES] = turned_ref[tile]


def component_chunk(blocks, flip, sent, so_far):
    devices, _, near, local, count, channels = sent.shape
    size = devices * near * count
    in_specs = [
        pl.BlockSpec(
            (devices, None, near, None, count, channels), lambda b, p, f: (0, b, 0, p, 0, 0)
        )
    ]
    args = [sent]
    aliases = {}
    if so_far is not None:
        in_specs.append(pl.BlockSpec(memory_space=pl.ANY))
        args.append(so_far)
        aliases = {2: 0}
    return call(
        functools.partial(output_kernel, channels // 4),
        0,
        8 * sent.size,
        args,
        grid=(len(blocks), local),
        in_specs=in_specs,
        out_specs=pl.BlockSpec(
            (None, channels, size), lambda b, p, f: (4 * p + blocks[0] + b, 0, 0)
        ),
        out_shape=jax.ShapeDtypeStruct((4 * local, channels, size), F32),
        scratch_shapes=[
            pltpu.VMEM((devices, near, count, channels), F32),
            pltpu.VMEM((size // LANES, channels, LANES), F32),
        ],
        scalars=(flip,),
        aliases=aliases,
    )


def exchange(values, pairs):
    devices, blocks, near, local, count, channels = values.shape
    sent = values.reshape(devices, blocks, near, local * count, channels)
    if not pairs:
        return lax.all_to_all(sent, "mom", split_axis=0, concat_axis=0, tiled=True)
    arrived = [sent]
    for s in range(1, devices):
        route = [(d, d ^ s) for d in range(devices)]
        arrived.append(lax.ppermute(sent[s : s + 1], "mom", route))
    return arrived


CHUNKS = (((0, 1), True), ((2, 3), False))


def shards(
    devices,
    source,
    green,
    couple_one,
    couple_two,
    p_bracket,
    q_bracket,
    p_weight,
    q_weight,
    qr_bracket,
    r_bracket,
    qr_weight,
    r_weight,
):
    rows_one, _, size_one = source.shape
    rows_two, size_two = green.shape
    near_r, near_p = rows_one // 4, rows_two // 4
    r_size, p_size = devices * near_r, devices * near_p
    q_size = size_one // p_size
    me = lax.axis_index("mom").astype(jnp.int32)
    flips = [jnp.stack([me if pairs else jnp.int32(0), me]) for _, pairs in CHUNKS]

    first_inputs = (p_bracket, q_bracket, p_weight, q_weight)

    def by_r(array):
        lead = array.shape[:-1]
        return array.reshape(lead + (q_size, r_size)).swapaxes(-1, -2).reshape(lead + (-1,))

    second_maps = spline_maps(
        by_r(r_bracket), by_r(qr_bracket), by_r(r_weight), by_r(qr_weight), q_size
    )
    green = green.reshape(near_p, 4, q_size, r_size).transpose(3, 2, 1, 0)
    green = green.reshape(size_two, 4 * near_p)
    arrived = []
    for step in range(ITERS):
        ones = []
        for flip, (blocks, pairs) in zip(flips, CHUNKS):
            if step == 0:
                if not ones:
                    one, *first_maps = first_one_building(
                        blocks, flip, source, couple_one, first_inputs, near_p, devices, q_size
                    )
                else:
                    one = first_one(blocks, flip, source, couple_one, first_maps, near_p, devices)
            else:
                one = later_one(blocks, flip, backs, couple_one, first_maps, near_p, devices)
            ones.append(exchange(one, pairs))
        arrived.append(ones)
        twos = []
        backs = []
        for n, (flip, (blocks, pairs)) in enumerate(zip(flips, CHUNKS)):
            chunks = [arrived[0][n]] + ([arrived[step][n]] if step else [])
            lanes = slice(blocks[0] * near_p, (blocks[-1] + 1) * near_p)
            scale = green[:, lanes]
            two = component_two(
                blocks, flip, chunks, couple_two, scale, second_maps, near_r, devices
            )
            twos.append(two)
            backs.append(exchange(two, pairs))
    component = amplitude = None
    for flip, (blocks, _), two, back in zip(flips, CHUNKS, twos, backs):
        component = component_chunk(blocks, flip, two, component)
        amplitude = amplitude_chunk(blocks, flip, source, back, amplitude)
    return amplitude, component


def whole_map(first, second, first_weight, second_weight, first_count, second_count):
    first_rows = jnp.zeros((first.shape[0], first_count), F32)
    second_rows = jnp.zeros((second.shape[0], second_count), F32)
    first_grid = jnp.arange(first_count, dtype=jnp.int32)[None, :] - first[:, None]
    second_grid = jnp.arange(second_count, dtype=jnp.int32)[None, :] - second[:, None]
    for offset in range(4):
        first_rows += jnp.where(first_grid == offset, first_weight[offset][:, None], 0.0)
        second_rows += jnp.where(second_grid == offset, second_weight[offset][:, None], 0.0)
    return (first_rows[:, :, None] * second_rows[:, None, :]).reshape(first.shape[0], -1)


def row_mats(couple, rows, start):
    select = jax.nn.one_hot((start + jnp.arange(rows, dtype=jnp.int32)) % 4, 4, dtype=F32)
    return jnp.einsum("rc,kcmn->krmn", select, couple, precision=lax.Precision.HIGHEST)


def mix_rows(mats, values):
    return jnp.einsum("rmn,rnx->rmx", mats, values, precision=lax.Precision.HIGHEST)


def interpolate_rows(values, matrix):
    return jnp.einsum("rcx,yx->rcy", values, matrix, precision=lax.Precision.HIGHEST)


def shards_by_row(
    devices,
    source,
    green,
    couple_one,
    couple_two,
    p_bracket,
    q_bracket,
    p_weight,
    q_weight,
    qr_bracket,
    r_bracket,
    qr_weight,
    r_weight,
):
    rows_one, channels, size_one = source.shape
    rows_two, size_two = green.shape
    angles = couple_one.shape[0]
    quarter = channels // 4
    r_size, p_size = devices * rows_one // 4, devices * rows_two // 4
    q_size = size_one // p_size
    here = lax.axis_index("mom")
    first = [
        whole_map(p_bracket[k], q_bracket[k], p_weight[k], q_weight[k], p_size, q_size)
        for k in range(angles)
    ]
    second = [
        whole_map(qr_bracket[k], r_bracket[k], qr_weight[k], r_weight[k], q_size, r_size)
        for k in range(angles)
    ]
    mats_one = row_mats(couple_one, rows_one, here * rows_one)
    mats_two = row_mats(couple_two, rows_two, here * rows_two)
    state = source
    for _ in range(ITERS):
        one = sum(interpolate_rows(mix_rows(mats_one[k], state), first[k]) for k in range(angles))
        sent = one.reshape(rows_one, 4, quarter, p_size, q_size).transpose(3, 1, 0, 2, 4)
        sent = sent.reshape(4 * p_size, rows_one, quarter * q_size)
        sent = lax.all_to_all(sent, "mom", split_axis=0, concat_axis=1, tiled=True)
        sent = sent.reshape(rows_two, r_size, 4, quarter, q_size).transpose(0, 3, 2, 4, 1)
        sent = sent.reshape(rows_two, channels, size_two)
        total = sum(mix_rows(mats_two[k], interpolate_rows(sent, second[k])) for k in range(angles))
        component = green[:, None, :] * total
        back = component.reshape(rows_two, quarter, 4, q_size, r_size).transpose(4, 2, 0, 1, 3)
        back = back.reshape(4 * r_size, rows_two, quarter * q_size)
        back = lax.all_to_all(back, "mom", split_axis=0, concat_axis=1, tiled=True)
        back = back.reshape(rows_one, p_size, 4, quarter, q_size).transpose(0, 2, 3, 1, 4)
        state = source + back.reshape(source.shape)
    return state, component


def solution(mesh):
    spread = ("energy", "mom")
    placed = (P(spread, None, None), P(spread, None)) + (P(),) * 10
    devices = mesh.shape["mom"]

    def body(source, green, *rest):
        whole_rows = source.shape[0] % 4 == 0 and green.shape[0] % 4 == 0
        chosen = shards if whole_rows and source.shape[1] == LANES else shards_by_row
        return chosen(devices, source, green, *rest)

    return jax.shard_map(
        body,
        mesh=mesh,
        in_specs=placed,
        out_specs=(P(spread, None, None), P(spread, None, None)),
        check_vma=False,
    )
```

profile of v0, /device:TPU:9, one launch (start us, length us, event | category | flops | bytes accessed | tf_op | source)
XLA Modules:
  0.0 571.0 jit_solution(17009209752591962371)
XLA Ops:
  1.9 18.6 %shard_map.131 = (f32[16,2,2,2,32,128]{5,4,3,2,1,0:T(8,128)}, bf16[1024,2048]{1,0:T(8,128)(2,1)}, bf16[1024,2048]{1,0:T(8,128)(2,1)}) custom-call(s32[2]{0:T(128)} %pad_add_fusion.1.flip_ref, f32[8,128,1024]{2,1,0:T(8,128)} %source_ref.7, f32[2,4,128,128]{3,2,1,0:T(8,128)} %refs_17_.3, s32[2,1024]{1,0:T(2,128)} %refs_0_.1, s32[2,1024]{1,0:T(2,128)} %refs_1_.2, ...), custom_call_target="tpu_custom_call" | custom-call | flops 7247757312 | bytes 12582912 | tf_op jit(solution)/shard_map/pallas_call | solution.py:35
  20.5 13.5 %shard_map.132 = f32[16,2,2,2,32,128]{5,4,3,2,1,0:T(8,128)} custom-call(s32[2]{0:T(128)} %pad_add_fusion.flip_ref, f32[8,128,1024]{2,1,0:T(8,128)} %source_ref.7, f32[2,4,128,128]{3,2,1,0:T(8,128)} %refs_17_.3, bf16[1024,2048]{1,0:T(8,128)(2,1)} %get-tuple-element.7.high_ref.refs_18_, bf16[1024,2048]{1,0:T(8,128)(2,1)} %get-tuple-element.8.low_ref.refs_19_), custom_call_target="tpu_custom_call" | custom-call | flops 7247757312 | bytes 12582912 | tf_op jit(solution)/shard_map/pallas_call | solution.py:35
  34.0 6.7 %all-to-all-start = ((f32[16,2,2,64,128]{4,3,2,1,0:T(8,128)}), f32[16,2,2,64,128]{4,3,2,1,0:T(8,128)S(1)}, u32[]{:S(2)}, u32[]{:S(2)}) async-start(f32[16,2,2,64,128]{4,3,2,1,0:T(8,128)} %bitcast.85), calls=%async_computation | async-start | bytes 4194304 | tf_op jit(solution)/shard_map/all_to_all | solution.py:642
  45.7 8.2 %shard_map.133 = (bf16[1024,2048]{1,0:T(8,128)(2,1)}, bf16[1024,2048]{1,0:T(8,128)(2,1)}) custom-call(s32[2,1024]{1,0:T(2,128)} %reshape.123.refs_0_, s32[2,1024]{1,0:T(2,128)} %reshape.125.refs_1_, f32[2,4,1024]{2,1,0:T(4,128)} %reshape.127.refs_2_, f32[2,4,1024]{2,1,0:T(4,128)} %reshape.129.refs_3_), custom_call_target="tpu_custom_call" | custom-call | flops 20971520 | bytes 8388608 | tf_op jit(solution)/shard_map/pallas_call | solution.py:35
  53.9 32.9 %all-to-all-done.refs_0_ = f32[16,2,2,64,128]{4,3,2,1,0:T(8,128)S(1)} async-done(((f32[16,2,2,64,128]{4,3,2,1,0:T(8,128)}), f32[16,2,2,64,128]{4,3,2,1,0:T(8,128)S(1)}, u32[]{:S(2)}, u32[]{:S(2)}) %all-to-all-start) | async-done | bytes 2097184 | tf_op jit(solution)/shard_map/all_to_all | solution.py:642
  88.2 14.4 %shard_map.135 = f32[16,2,2,2,32,128]{5,4,3,2,1,0:T(8,128)} custom-call(s32[2]{0:T(128)} %pad_add_fusion.flip_ref, f32[16,2,2,64,128]{4,3,2,1,0:T(8,128)} %copy-done.1, f32[2,4,128,128]{3,2,1,0:T(8,128)} %refs_32_.1, f32[1024,4]{1,0:T(8,128)} %copy.29.refs_2_.refs_3_, bf16[1024,2048]{1,0:T(8,128)(2,1)} %get-tuple-element.10.refs_18_.refs_3_.refs_4_.refs_34_, ...), custom_call_target="tpu_custom_call" | custom-call | flops 7247757312 | bytes 10485760 | tf_op jit(solution)/shard_map/pallas_call | solution.py:35
  102.5 6.1 %all-to-all-start.1 = ((f32[16,2,2,64,128]{4,3,2,1,0:T(8,128)}), f32[16,2,2,64,128]{4,3,2,1,0:T(8,128)S(1)}, u32[]{:S(2)}, u32[]{:S(2)}) async-start(f32[16,2,2,64,128]{4,3,2,1,0:T(8,128)} %bitcast.84), calls=%async_computation.1 | async-start | bytes 4194304 | tf_op jit(solution)/shard_map/all_to_all | solution.py:642
  114.6 7.4 %collective-permute-start.10 = (f32[1,2,2,64,128]{4,3,2,1,0:T(8,128)S(1)}, f32[1,2,2,64,128]{4,3,2,1,0:T(8,128)S(1)}, u32[]{:S(2)}, u32[]{:S(2)}) collective-permute-start(f32[1,2,2,64,128]{4,3,2,1,0:T(8,128)S(1)} %bitcast.130), channel_id=1, source_target_pairs={{0,11},{1,10},{2,9},{3,8},{4,15},{5,14},{6,13},{7,12},{8,3},{9,2},... | collective-permute-start | bytes 393224 | tf_op jit(solution)/shard_map/ppermute | solution.py:646
  122.0 51.5 %collective-permute-done.13.refs_14_ = f32[1,2,2,64,128]{4,3,2,1,0:T(8,128)S(1)} collective-permute-done((f32[1,2,2,64,128]{4,3,2,1,0:T(8,128)S(1)}, f32[1,2,2,64,128]{4,3,2,1,0:T(8,128)S(1)}, u32[]{:S(2)}, u32[]{:S(2)}) %collective-permute-start.13) | collective-permute-done | bytes 131104 | tf_op jit(solution)/shard_map/ppermute | solution.py:646
  173.6 3.7 collective-permute-done.14.refs_15_
  177.6 7.1 %collective-permute-done.12.refs_13_ = f32[1,2,2,64,128]{4,3,2,1,0:T(8,128)S(1)} collective-permute-done((f32[1,2,2,64,128]{4,3,2,1,0:T(8,128)S(1)}, f32[1,2,2,64,128]{4,3,2,1,0:T(8,128)S(1)}, u32[]{:S(2)}, u32[]{:S(2)}) %collective-permute-start.12) | collective-permute-done | bytes 131104 | tf_op jit(solution)/shard_map/ppermute | solution.py:646
  186.9 3.4 collective-permute-done.10.refs_11_
  190.3 5.0 collective-permute-start.5
  195.3 3.4 collective-permute-start.4
  206.0 2.8 collective-permute-done.3.refs_4_
  208.8 14.6 %shard_map.134 = f32[16,2,2,2,32,128]{5,4,3,2,1,0:T(8,128)} custom-call(s32[2]{0:T(128)} %pad_add_fusion.1.flip_ref, f32[16,2,2,64,128]{4,3,2,1,0:T(8,128)} %bitcast.87, f32[1,2,2,64,128]{4,3,2,1,0:T(8,128)} %collective-permute-done.refs_1_, f32[1,2,2,64,128]{4,3,2,1,0:T(8,128)} %collective-permute-done.1.refs_2_, ...), custom_call_target="tpu_custom_call" | custom-call | flops 7247757312 | bytes 10485760 | tf_op jit(solution)/shard_map/pallas_call | solution.py:35
  229.3 8.3 %collective-permute-start.25 = (f32[1,2,2,64,128]{4,3,2,1,0:T(8,128)S(1)}, f32[1,2,2,64,128]{4,3,2,1,0:T(8,128)S(1)}, u32[]{:S(2)}, u32[]{:S(2)}) collective-permute-start(f32[1,2,2,64,128]{4,3,2,1,0:T(8,128)S(1)} %bitcast.131), channel_id=1, source_target_pairs={{0,11},{1,10},{2,9},{3,8},{4,15},{5,14},{6,13},{7,12},{8,3},{9,2},... | collective-permute-start | bytes 393224 | tf_op jit(solution)/shard_map/ppermute | solution.py:646
  237.6 14.2 %collective-permute-done.29.refs_15_ = f32[1,2,2,64,128]{4,3,2,1,0:T(8,128)S(1)} collective-permute-done((f32[1,2,2,64,128]{4,3,2,1,0:T(8,128)S(1)}, f32[1,2,2,64,128]{4,3,2,1,0:T(8,128)S(1)}, u32[]{:S(2)}, u32[]{:S(2)}) %collective-permute-start.29) | collective-permute-done | bytes 131104 | tf_op jit(solution)/shard_map/ppermute | solution.py:646
  251.8 7.1 %collective-permute-done.27.refs_13_ = f32[1,2,2,64,128]{4,3,2,1,0:T(8,128)S(1)} collective-permute-done((f32[1,2,2,64,128]{4,3,2,1,0:T(8,128)S(1)}, f32[1,2,2,64,128]{4,3,2,1,0:T(8,128)S(1)}, u32[]{:S(2)}, u32[]{:S(2)}) %collective-permute-start.27) | collective-permute-done | bytes 131104 | tf_op jit(solution)/shard_map/ppermute | solution.py:646
  262.6 5.5 collective-permute-start.20
  268.1 2.4 collective-permute-start.19
  275.7 3.0 collective-permute-start.15
  278.7 2.6 collective-permute-done.18.refs_4_
  284.0 16.8 %shard_map.136 = f32[16,2,2,2,32,128]{5,4,3,2,1,0:T(8,128)} custom-call(s32[2]{0:T(128)} %pad_add_fusion.flip_ref, f32[16,2,2,64,128]{4,3,2,1,0:T(8,128)} %bitcast.90, f32[1,2,2,64,128]{4,3,2,1,0:T(8,128)} %collective-permute-done.15.refs_1_, f32[1,2,2,64,128]{4,3,2,1,0:T(8,128)} %copy-done.59, f32[1,2,2,64,128]{4,3,2,1,0:T(8,128)} %copy-done.57, ...), custom_call_target="tpu_custom_call" | custom-call | flops 9663676416 | bytes 12582912 | tf_op jit(solution)/shard_map/pallas_call | solution.py:35
  300.7 56.0 %all_to_all.20.refs_1_ = f32[16,2,2,64,128]{4,3,2,1,0:T(8,128)} all-to-all(f32[16,2,2,64,128]{4,3,2,1,0:T(8,128)} %bitcast.86), channel_id=1, replica_groups=mesh['energy'=2,'mom'=16] {'mom'}, dimensions={0} | all-to-all | bytes 4194304 | tf_op jit(solution)/shard_map/all_to_all | solution.py:642
  356.7 15.0 %shard_map.137.sent_ref = f32[16,2,2,2,32,128]{5,4,3,2,1,0:T(8,128)} custom-call(s32[2]{0:T(128)} %pad_add_fusion.flip_ref, f32[16,2,2,64,128]{4,3,2,1,0:T(8,128)} %copy-done.1, f32[16,2,2,64,128]{4,3,2,1,0:T(8,128)} %all_to_all.20.refs_1_, f32[2,4,128,128]{3,2,1,0:T(8,128)} %refs_32_.1, f32[1024,4]{1,0:T(8,128)} %copy.29.refs_2_.refs_3_, ...), custom_call_target="tpu_custom_call" | custom-call | flops 7247757312 | bytes 12582912 | tf_op jit(solution)/shard_map/pallas_call | solution.py:35
  371.7 4.3 all-to-all-start.3
  376.0 16.7 %shard_map.138 = f32[16,2,2,2,32,128]{5,4,3,2,1,0:T(8,128)} custom-call(s32[2]{0:T(128)} %pad_add_fusion.1.flip_ref, f32[16,2,2,64,128]{4,3,2,1,0:T(8,128)} %bitcast.91, f32[1,2,2,64,128]{4,3,2,1,0:T(8,128)} %collective-permute-done.15.refs_1_, f32[1,2,2,64,128]{4,3,2,1,0:T(8,128)} %copy-done.59, f32[1,2,2,64,128]{4,3,2,1,0:T(8,128)} %copy-done.57, ...), custom_call_target="tpu_custom_call" | custom-call | flops 9663676416 | bytes 12582912 | tf_op jit(solution)/shard_map/pallas_call | solution.py:35
  398.7 7.4 %collective-permute-start.40 = (f32[1,2,2,64,128]{4,3,2,1,0:T(8,128)S(1)}, f32[1,2,2,64,128]{4,3,2,1,0:T(8,128)S(1)}, u32[]{:S(2)}, u32[]{:S(2)}) collective-permute-start(f32[1,2,2,64,128]{4,3,2,1,0:T(8,128)S(1)} %bitcast.132), channel_id=1, source_target_pairs={{0,11},{1,10},{2,9},{3,8},{4,15},{5,14},{6,13},{7,12},{8,3},{9,2},... | collective-permute-start | bytes 393224 | tf_op jit(solution)/shard_map/ppermute | solution.py:646
  406.1 34.8 %collective-permute-done.43.refs_30_ = f32[1,2,2,64,128]{4,3,2,1,0:T(8,128)S(1)} collective-permute-done((f32[1,2,2,64,128]{4,3,2,1,0:T(8,128)S(1)}, f32[1,2,2,64,128]{4,3,2,1,0:T(8,128)S(1)}, u32[]{:S(2)}, u32[]{:S(2)}) %collective-permute-start.43) | collective-permute-done | bytes 131104 | tf_op jit(solution)/shard_map/ppermute | solution.py:646
  440.9 3.7 collective-permute-done.44.refs_31_
  445.0 7.1 %collective-permute-done.42.refs_29_ = f32[1,2,2,64,128]{4,3,2,1,0:T(8,128)S(1)} collective-permute-done((f32[1,2,2,64,128]{4,3,2,1,0:T(8,128)S(1)}, f32[1,2,2,64,128]{4,3,2,1,0:T(8,128)S(1)}, u32[]{:S(2)}, u32[]{:S(2)}) %collective-permute-start.42) | collective-permute-done | bytes 131104 | tf_op jit(solution)/shard_map/ppermute | solution.py:646
  454.3 3.4 collective-permute-done.40.refs_27_
  457.7 5.0 collective-permute-start.35
  462.7 3.4 collective-permute-start.34
  473.3 2.8 collective-permute-done.33.refs_20_
  476.9 15.1 %shard_map.139.sent_ref = f32[16,2,2,2,32,128]{5,4,3,2,1,0:T(8,128)} custom-call(s32[2]{0:T(128)} %pad_add_fusion.1.flip_ref, f32[16,2,2,64,128]{4,3,2,1,0:T(8,128)} %bitcast.88, f32[1,2,2,64,128]{4,3,2,1,0:T(8,128)} %collective-permute-done.refs_1_, f32[1,2,2,64,128]{4,3,2,1,0:T(8,128)} %collective-permute-done.1.refs_2_, ...), custom_call_target="tpu_custom_call" | custom-call | flops 7247757312 | bytes 12582912 | tf_op jit(solution)/shard_map/pallas_call | solution.py:35
  492.0 2.5 fusion
  498.6 8.1 %collective-permute-start.55 = (f32[1,2,2,64,128]{4,3,2,1,0:T(8,128)S(1)}, f32[1,2,2,64,128]{4,3,2,1,0:T(8,128)S(1)}, u32[]{:S(2)}, u32[]{:S(2)}) collective-permute-start(f32[1,2,2,64,128]{4,3,2,1,0:T(8,128)S(1)} %bitcast.133), channel_id=1, source_target_pairs={{0,11},{1,10},{2,9},{3,8},{4,15},{5,14},{6,13},{7,12},{8,3},{9,2},... | collective-permute-start | bytes 393224 | tf_op jit(solution)/shard_map/ppermute | solution.py:646
  506.7 14.4 %collective-permute-done.59.refs_15_ = f32[1,2,2,64,128]{4,3,2,1,0:T(8,128)S(1)} collective-permute-done((f32[1,2,2,64,128]{4,3,2,1,0:T(8,128)S(1)}, f32[1,2,2,64,128]{4,3,2,1,0:T(8,128)S(1)}, u32[]{:S(2)}, u32[]{:S(2)}) %collective-permute-start.59) | collective-permute-done | bytes 131104 | tf_op jit(solution)/shard_map/ppermute | solution.py:646
  521.1 7.2 %collective-permute-done.57.refs_13_ = f32[1,2,2,64,128]{4,3,2,1,0:T(8,128)S(1)} collective-permute-done((f32[1,2,2,64,128]{4,3,2,1,0:T(8,128)S(1)}, f32[1,2,2,64,128]{4,3,2,1,0:T(8,128)S(1)}, u32[]{:S(2)}, u32[]{:S(2)}) %collective-permute-start.57) | collective-permute-done | bytes 131104 | tf_op jit(solution)/shard_map/ppermute | solution.py:646
  531.7 5.7 %collective-permute-start.50 = (f32[1,2,2,64,128]{4,3,2,1,0:T(8,128)S(1)}, f32[1,2,2,64,128]{4,3,2,1,0:T(8,128)S(1)}, u32[]{:S(2)}, u32[]{:S(2)}) collective-permute-start(f32[1,2,2,64,128]{4,3,2,1,0:T(8,128)S(1)} %bitcast.113), channel_id=1, source_target_pairs={{0,6},{1,7},{2,4},{3,5},{4,2},{5,3},{6,0},{7,1},{8,14},{9,15},{10,... | collective-permute-start | bytes 393224 | tf_op jit(solution)/shard_map/ppermute | solution.py:646
  537.4 2.4 collective-permute-start.49
  544.9 3.0 collective-permute-start.45
  548.0 5.3 shard_map.142.refs_0_
  554.2 5.0 shard_map.140.refs_1_
  559.2 5.3 shard_map.143
  565.8 5.2 shard_map.141
  (240 shorter events, 71.6 us)
Async XLA Ops:
  34.0 52.8 %all-to-all-start = ((f32[16,2,2,64,128]{4,3,2,1,0:T(8,128)}), f32[16,2,2,64,128]{4,3,2,1,0:T(8,128)S(1)}, u32[]{:S(2)}, u32[]{:S(2)}) async-start(f32[16,2,2,64,128]{4,3,2,1,0:T(8,128)} %bitcast.85), calls=%async_computation | async-start | bytes 4194304 | tf_op jit(solution)/shard_map/all_to_all | solution.py:642
  102.5 180.1 %all-to-all-start.1 = ((f32[16,2,2,64,128]{4,3,2,1,0:T(8,128)}), f32[16,2,2,64,128]{4,3,2,1,0:T(8,128)S(1)}, u32[]{:S(2)}, u32[]{:S(2)}) async-start(f32[16,2,2,64,128]{4,3,2,1,0:T(8,128)} %bitcast.84), calls=%async_computation.1 | async-start | bytes 4194304 | tf_op jit(solution)/shard_map/all_to_all | solution.py:642
  110.4 63.1 %collective-permute-start.13 = (f32[1,2,2,64,128]{4,3,2,1,0:T(8,128)S(1)}, f32[1,2,2,64,128]{4,3,2,1,0:T(8,128)S(1)}, u32[]{:S(2)}, u32[]{:S(2)}) collective-permute-start(f32[1,2,2,64,128]{4,3,2,1,0:T(8,128)S(1)} %bitcast.146), channel_id=1, source_target_pairs={{0,14},{1,15},{2,12},{3,13},{4,10},{5,11},{6,8},{7,9},{8,6},{9,7},... | collective-permute-start | bytes 393224 | tf_op jit(solution)/shard_map/ppermute | solution.py:646
  112.6 64.7 %collective-permute-start.14 = (f32[1,2,2,64,128]{4,3,2,1,0:T(8,128)S(1)}, f32[1,2,2,64,128]{4,3,2,1,0:T(8,128)S(1)}, u32[]{:S(2)}, u32[]{:S(2)}) collective-permute-start(f32[1,2,2,64,128]{4,3,2,1,0:T(8,128)S(1)} %bitcast.142), channel_id=1, source_target_pairs={{0,15},{1,14},{2,13},{3,12},{4,11},{5,10},{6,9},{7,8},{8,7},{9,6},... | collective-permute-start | bytes 393224 | tf_op jit(solution)/shard_map/ppermute | solution.py:646
  113.4 71.3 %collective-permute-start.12 = (f32[1,2,2,64,128]{4,3,2,1,0:T(8,128)S(1)}, f32[1,2,2,64,128]{4,3,2,1,0:T(8,128)S(1)}, u32[]{:S(2)}, u32[]{:S(2)}) collective-permute-start(f32[1,2,2,64,128]{4,3,2,1,0:T(8,128)S(1)} %bitcast.138), channel_id=1, source_target_pairs={{0,13},{1,12},{2,15},{3,14},{4,9},{5,8},{6,11},{7,10},{8,5},{9,4},... | collective-permute-start | bytes 393224 | tf_op jit(solution)/shard_map/ppermute | solution.py:646
  114.3 72.3 %collective-permute-start.11 = (f32[1,2,2,64,128]{4,3,2,1,0:T(8,128)S(1)}, f32[1,2,2,64,128]{4,3,2,1,0:T(8,128)S(1)}, u32[]{:S(2)}, u32[]{:S(2)}) collective-permute-start(f32[1,2,2,64,128]{4,3,2,1,0:T(8,128)S(1)} %bitcast.134), channel_id=1, source_target_pairs={{0,12},{1,13},{2,14},{3,15},{4,8},{5,9},{6,10},{7,11},{8,4},{9,5},... | collective-permute-start | bytes 393224 | tf_op jit(solution)/shard_map/ppermute | solution.py:646
  114.6 75.8 %collective-permute-start.10 = (f32[1,2,2,64,128]{4,3,2,1,0:T(8,128)S(1)}, f32[1,2,2,64,128]{4,3,2,1,0:T(8,128)S(1)}, u32[]{:S(2)}, u32[]{:S(2)}) collective-permute-start(f32[1,2,2,64,128]{4,3,2,1,0:T(8,128)S(1)} %bitcast.130), channel_id=1, source_target_pairs={{0,11},{1,10},{2,9},{3,8},{4,15},{5,14},{6,13},{7,12},{8,3},{9,2},... | collective-permute-start | bytes 393224 | tf_op jit(solution)/shard_map/ppermute | solution.py:646
  173.6 21.7 %collective-permute-start.9 = (f32[1,2,2,64,128]{4,3,2,1,0:T(8,128)S(1)}, f32[1,2,2,64,128]{4,3,2,1,0:T(8,128)S(1)}, u32[]{:S(2)}, u32[]{:S(2)}) collective-permute-start(f32[1,2,2,64,128]{4,3,2,1,0:T(8,128)S(1)} %bitcast.126), channel_id=1, source_target_pairs={{0,10},{1,11},{2,8},{3,9},{4,14},{5,15},{6,12},{7,13},{8,2},{9,3},... | collective-permute-start | bytes 393224 | tf_op jit(solution)/shard_map/ppermute | solution.py:646
  177.2 21.5 %collective-permute-start.8 = (f32[1,2,2,64,128]{4,3,2,1,0:T(8,128)S(1)}, f32[1,2,2,64,128]{4,3,2,1,0:T(8,128)S(1)}, u32[]{:S(2)}, u32[]{:S(2)}) collective-permute-start(f32[1,2,2,64,128]{4,3,2,1,0:T(8,128)S(1)} %bitcast.122), channel_id=1, source_target_pairs={{0,9},{1,8},{2,11},{3,10},{4,13},{5,12},{6,15},{7,14},{8,1},{9,0},... | collective-permute-start | bytes 393224 | tf_op jit(solution)/shard_map/ppermute | solution.py:646
  184.7 15.3 %collective-permute-start.7 = (f32[1,2,2,64,128]{4,3,2,1,0:T(8,128)S(1)}, f32[1,2,2,64,128]{4,3,2,1,0:T(8,128)S(1)}, u32[]{:S(2)}, u32[]{:S(2)}) collective-permute-start(f32[1,2,2,64,128]{4,3,2,1,0:T(8,128)S(1)} %bitcast.118), channel_id=1, source_target_pairs={{0,8},{1,9},{2,10},{3,11},{4,12},{5,13},{6,14},{7,15},{8,0},{9,1},... | collective-permute-start | bytes 393224 | tf_op jit(solution)/shard_map/ppermute | solution.py:646
  186.6 14.3 %collective-permute-start.6 = (f32[1,2,2,64,128]{4,3,2,1,0:T(8,128)S(1)}, f32[1,2,2,64,128]{4,3,2,1,0:T(8,128)S(1)}, u32[]{:S(2)}, u32[]{:S(2)}) collective-permute-start(f32[1,2,2,64,128]{4,3,2,1,0:T(8,128)S(1)} %bitcast.114), channel_id=1, source_target_pairs={{0,7},{1,6},{2,5},{3,4},{4,3},{5,2},{6,1},{7,0},{8,15},{9,14},{10,... | collective-permute-start | bytes 393224 | tf_op jit(solution)/shard_map/ppermute | solution.py:646
  190.3 12.8 %collective-permute-start.5 = (f32[1,2,2,64,128]{4,3,2,1,0:T(8,128)S(1)}, f32[1,2,2,64,128]{4,3,2,1,0:T(8,128)S(1)}, u32[]{:S(2)}, u32[]{:S(2)}) collective-permute-start(f32[1,2,2,64,128]{4,3,2,1,0:T(8,128)S(1)} %bitcast.110), channel_id=1, source_target_pairs={{0,6},{1,7},{2,4},{3,5},{4,2},{5,3},{6,0},{7,1},{8,14},{9,15},{10,... | collective-permute-start | bytes 393224 | tf_op jit(solution)/shard_map/ppermute | solution.py:646
  225.1 12.5 %collective-permute-start.28 = (f32[1,2,2,64,128]{4,3,2,1,0:T(8,128)S(1)}, f32[1,2,2,64,128]{4,3,2,1,0:T(8,128)S(1)}, u32[]{:S(2)}, u32[]{:S(2)}) collective-permute-start(f32[1,2,2,64,128]{4,3,2,1,0:T(8,128)S(1)} %bitcast.147), channel_id=1, source_target_pairs={{0,14},{1,15},{2,12},{3,13},{4,10},{5,11},{6,8},{7,9},{8,6},{9,7},... | collective-permute-start | bytes 393224 | tf_op jit(solution)/shard_map/ppermute | solution.py:646
  226.5 25.3 %collective-permute-start.29 = (f32[1,2,2,64,128]{4,3,2,1,0:T(8,128)S(1)}, f32[1,2,2,64,128]{4,3,2,1,0:T(8,128)S(1)}, u32[]{:S(2)}, u32[]{:S(2)}) collective-permute-start(f32[1,2,2,64,128]{4,3,2,1,0:T(8,128)S(1)} %bitcast.143), channel_id=1, source_target_pairs={{0,15},{1,14},{2,13},{3,12},{4,11},{5,10},{6,9},{7,8},{8,7},{9,6},... | collective-permute-start | bytes 393224 | tf_op jit(solution)/shard_map/ppermute | solution.py:646
  228.1 30.9 %collective-permute-start.27 = (f32[1,2,2,64,128]{4,3,2,1,0:T(8,128)S(1)}, f32[1,2,2,64,128]{4,3,2,1,0:T(8,128)S(1)}, u32[]{:S(2)}, u32[]{:S(2)}) collective-permute-start(f32[1,2,2,64,128]{4,3,2,1,0:T(8,128)S(1)} %bitcast.139), channel_id=1, source_target_pairs={{0,13},{1,12},{2,15},{3,14},{4,9},{5,8},{6,11},{7,10},{8,5},{9,4},... | collective-permute-start | bytes 393224 | tf_op jit(solution)/shard_map/ppermute | solution.py:646
  228.2 32.1 %collective-permute-start.26 = (f32[1,2,2,64,128]{4,3,2,1,0:T(8,128)S(1)}, f32[1,2,2,64,128]{4,3,2,1,0:T(8,128)S(1)}, u32[]{:S(2)}, u32[]{:S(2)}) collective-permute-start(f32[1,2,2,64,128]{4,3,2,1,0:T(8,128)S(1)} %bitcast.135), channel_id=1, source_target_pairs={{0,12},{1,13},{2,14},{3,15},{4,8},{5,9},{6,10},{7,11},{8,4},{9,5},... | collective-permute-start | bytes 393224 | tf_op jit(solution)/shard_map/ppermute | solution.py:646
  229.3 33.3 %collective-permute-start.25 = (f32[1,2,2,64,128]{4,3,2,1,0:T(8,128)S(1)}, f32[1,2,2,64,128]{4,3,2,1,0:T(8,128)S(1)}, u32[]{:S(2)}, u32[]{:S(2)}) collective-permute-start(f32[1,2,2,64,128]{4,3,2,1,0:T(8,128)S(1)} %bitcast.131), channel_id=1, source_target_pairs={{0,11},{1,10},{2,9},{3,8},{4,15},{5,14},{6,13},{7,12},{8,3},{9,2},... | collective-permute-start | bytes 393224 | tf_op jit(solution)/shard_map/ppermute | solution.py:646
  237.6 30.5 %collective-permute-start.24 = (f32[1,2,2,64,128]{4,3,2,1,0:T(8,128)S(1)}, f32[1,2,2,64,128]{4,3,2,1,0:T(8,128)S(1)}, u32[]{:S(2)}, u32[]{:S(2)}) collective-permute-start(f32[1,2,2,64,128]{4,3,2,1,0:T(8,128)S(1)} %bitcast.127), channel_id=1, source_target_pairs={{0,10},{1,11},{2,8},{3,9},{4,14},{5,15},{6,12},{7,13},{8,2},{9,3},... | collective-permute-start | bytes 393224 | tf_op jit(solution)/shard_map/ppermute | solution.py:646
  251.8 18.7 %collective-permute-start.23 = (f32[1,2,2,64,128]{4,3,2,1,0:T(8,128)S(1)}, f32[1,2,2,64,128]{4,3,2,1,0:T(8,128)S(1)}, u32[]{:S(2)}, u32[]{:S(2)}) collective-permute-start(f32[1,2,2,64,128]{4,3,2,1,0:T(8,128)S(1)} %bitcast.123), channel_id=1, source_target_pairs={{0,9},{1,8},{2,11},{3,10},{4,13},{5,12},{6,15},{7,14},{8,1},{9,0},... | collective-permute-start | bytes 393224 | tf_op jit(solution)/shard_map/ppermute | solution.py:646
  259.0 13.8 %collective-permute-start.22 = (f32[1,2,2,64,128]{4,3,2,1,0:T(8,128)S(1)}, f32[1,2,2,64,128]{4,3,2,1,0:T(8,128)S(1)}, u32[]{:S(2)}, u32[]{:S(2)}) collective-permute-start(f32[1,2,2,64,128]{4,3,2,1,0:T(8,128)S(1)} %bitcast.119), channel_id=1, source_target_pairs={{0,8},{1,9},{2,10},{3,11},{4,12},{5,13},{6,14},{7,15},{8,0},{9,1},... | collective-permute-start | bytes 393224 | tf_op jit(solution)/shard_map/ppermute | solution.py:646
  260.3 12.5 %collective-permute-start.21 = (f32[1,2,2,64,128]{4,3,2,1,0:T(8,128)S(1)}, f32[1,2,2,64,128]{4,3,2,1,0:T(8,128)S(1)}, u32[]{:S(2)}, u32[]{:S(2)}) collective-permute-start(f32[1,2,2,64,128]{4,3,2,1,0:T(8,128)S(1)} %bitcast.115), channel_id=1, source_target_pairs={{0,7},{1,6},{2,5},{3,4},{4,3},{5,2},{6,1},{7,0},{8,15},{9,14},{10,... | collective-permute-start | bytes 393224 | tf_op jit(solution)/shard_map/ppermute | solution.py:646
  262.6 13.1 %collective-permute-start.20 = (f32[1,2,2,64,128]{4,3,2,1,0:T(8,128)S(1)}, f32[1,2,2,64,128]{4,3,2,1,0:T(8,128)S(1)}, u32[]{:S(2)}, u32[]{:S(2)}) collective-permute-start(f32[1,2,2,64,128]{4,3,2,1,0:T(8,128)S(1)} %bitcast.111), channel_id=1, source_target_pairs={{0,6},{1,7},{2,4},{3,5},{4,2},{5,3},{6,0},{7,1},{8,14},{9,15},{10,... | collective-permute-start | bytes 393224 | tf_op jit(solution)/shard_map/ppermute | solution.py:646
  270.5 10.7 %collective-permute-start.18 = (f32[1,2,2,64,128]{4,3,2,1,0:T(8,128)S(1)}, f32[1,2,2,64,128]{4,3,2,1,0:T(8,128)S(1)}, u32[]{:S(2)}, u32[]{:S(2)}) collective-permute-start(f32[1,2,2,64,128]{4,3,2,1,0:T(8,128)S(1)} %bitcast.106), channel_id=1, source_target_pairs={{0,4},{1,5},{2,6},{3,7},{4,0},{5,1},{6,2},{7,3},{8,12},{9,13},{10,... | collective-permute-start | bytes 393224 | tf_op jit(solution)/shard_map/ppermute | solution.py:646
  371.7 192.8 %all-to-all-start.3 = ((f32[16,2,2,64,128]{4,3,2,1,0:T(8,128)}), f32[16,2,2,64,128]{4,3,2,1,0:T(8,128)S(1)}, u32[]{:S(2)}, u32[]{:S(2)}) async-start(f32[16,2,2,64,128]{4,3,2,1,0:T(8,128)} %bitcast.83), calls=%async_computation.3 | async-start | bytes 4194304 | tf_op jit(solution)/shard_map/all_to_all | solution.py:642
  394.5 46.4 %collective-permute-start.43 = (f32[1,2,2,64,128]{4,3,2,1,0:T(8,128)S(1)}, f32[1,2,2,64,128]{4,3,2,1,0:T(8,128)S(1)}, u32[]{:S(2)}, u32[]{:S(2)}) collective-permute-start(f32[1,2,2,64,128]{4,3,2,1,0:T(8,128)S(1)} %bitcast.148), channel_id=1, source_target_pairs={{0,14},{1,15},{2,12},{3,13},{4,10},{5,11},{6,8},{7,9},{8,6},{9,7},... | collective-permute-start | bytes 393224 | tf_op jit(solution)/shard_map/ppermute | solution.py:646
  396.7 47.9 %collective-permute-start.44 = (f32[1,2,2,64,128]{4,3,2,1,0:T(8,128)S(1)}, f32[1,2,2,64,128]{4,3,2,1,0:T(8,128)S(1)}, u32[]{:S(2)}, u32[]{:S(2)}) collective-permute-start(f32[1,2,2,64,128]{4,3,2,1,0:T(8,128)S(1)} %bitcast.144), channel_id=1, source_target_pairs={{0,15},{1,14},{2,13},{3,12},{4,11},{5,10},{6,9},{7,8},{8,7},{9,6},... | collective-permute-start | bytes 393224 | tf_op jit(solution)/shard_map/ppermute | solution.py:646
  397.5 54.6 %collective-permute-start.42 = (f32[1,2,2,64,128]{4,3,2,1,0:T(8,128)S(1)}, f32[1,2,2,64,128]{4,3,2,1,0:T(8,128)S(1)}, u32[]{:S(2)}, u32[]{:S(2)}) collective-permute-start(f32[1,2,2,64,128]{4,3,2,1,0:T(8,128)S(1)} %bitcast.140), channel_id=1, source_target_pairs={{0,13},{1,12},{2,15},{3,14},{4,9},{5,8},{6,11},{7,10},{8,5},{9,4},... | collective-permute-start | bytes 393224 | tf_op jit(solution)/shard_map/ppermute | solution.py:646
  398.4 55.6 %collective-permute-start.41 = (f32[1,2,2,64,128]{4,3,2,1,0:T(8,128)S(1)}, f32[1,2,2,64,128]{4,3,2,1,0:T(8,128)S(1)}, u32[]{:S(2)}, u32[]{:S(2)}) collective-permute-start(f32[1,2,2,64,128]{4,3,2,1,0:T(8,128)S(1)} %bitcast.136), channel_id=1, source_target_pairs={{0,12},{1,13},{2,14},{3,15},{4,8},{5,9},{6,10},{7,11},{8,4},{9,5},... | collective-permute-start | bytes 393224 | tf_op jit(solution)/shard_map/ppermute | solution.py:646
  398.7 59.0 %collective-permute-start.40 = (f32[1,2,2,64,128]{4,3,2,1,0:T(8,128)S(1)}, f32[1,2,2,64,128]{4,3,2,1,0:T(8,128)S(1)}, u32[]{:S(2)}, u32[]{:S(2)}) collective-permute-start(f32[1,2,2,64,128]{4,3,2,1,0:T(8,128)S(1)} %bitcast.132), channel_id=1, source_target_pairs={{0,11},{1,10},{2,9},{3,8},{4,15},{5,14},{6,13},{7,12},{8,3},{9,2},... | collective-permute-start | bytes 393224 | tf_op jit(solution)/shard_map/ppermute | solution.py:646
  440.9 21.7 %collective-permute-start.39 = (f32[1,2,2,64,128]{4,3,2,1,0:T(8,128)S(1)}, f32[1,2,2,64,128]{4,3,2,1,0:T(8,128)S(1)}, u32[]{:S(2)}, u32[]{:S(2)}) collective-permute-start(f32[1,2,2,64,128]{4,3,2,1,0:T(8,128)S(1)} %bitcast.128), channel_id=1, source_target_pairs={{0,10},{1,11},{2,8},{3,9},{4,14},{5,15},{6,12},{7,13},{8,2},{9,3},... | collective-permute-start | bytes 393224 | tf_op jit(solution)/shard_map/ppermute | solution.py:646
  444.6 21.5 %collective-permute-start.38 = (f32[1,2,2,64,128]{4,3,2,1,0:T(8,128)S(1)}, f32[1,2,2,64,128]{4,3,2,1,0:T(8,128)S(1)}, u32[]{:S(2)}, u32[]{:S(2)}) collective-permute-start(f32[1,2,2,64,128]{4,3,2,1,0:T(8,128)S(1)} %bitcast.124), channel_id=1, source_target_pairs={{0,9},{1,8},{2,11},{3,10},{4,13},{5,12},{6,15},{7,14},{8,1},{9,0},... | collective-permute-start | bytes 393224 | tf_op jit(solution)/shard_map/ppermute | solution.py:646
  452.1 15.3 %collective-permute-start.37 = (f32[1,2,2,64,128]{4,3,2,1,0:T(8,128)S(1)}, f32[1,2,2,64,128]{4,3,2,1,0:T(8,128)S(1)}, u32[]{:S(2)}, u32[]{:S(2)}) collective-permute-start(f32[1,2,2,64,128]{4,3,2,1,0:T(8,128)S(1)} %bitcast.120), channel_id=1, source_target_pairs={{0,8},{1,9},{2,10},{3,11},{4,12},{5,13},{6,14},{7,15},{8,0},{9,1},... | collective-permute-start | bytes 393224 | tf_op jit(solution)/shard_map/ppermute | solution.py:646
  454.0 14.3 %collective-permute-start.36 = (f32[1,2,2,64,128]{4,3,2,1,0:T(8,128)S(1)}, f32[1,2,2,64,128]{4,3,2,1,0:T(8,128)S(1)}, u32[]{:S(2)}, u32[]{:S(2)}) collective-permute-start(f32[1,2,2,64,128]{4,3,2,1,0:T(8,128)S(1)} %bitcast.116), channel_id=1, source_target_pairs={{0,7},{1,6},{2,5},{3,4},{4,3},{5,2},{6,1},{7,0},{8,15},{9,14},{10,... | collective-permute-start | bytes 393224 | tf_op jit(solution)/shard_map/ppermute | solution.py:646
  457.7 12.8 %collective-permute-start.35 = (f32[1,2,2,64,128]{4,3,2,1,0:T(8,128)S(1)}, f32[1,2,2,64,128]{4,3,2,1,0:T(8,128)S(1)}, u32[]{:S(2)}, u32[]{:S(2)}) collective-permute-start(f32[1,2,2,64,128]{4,3,2,1,0:T(8,128)S(1)} %bitcast.112), channel_id=1, source_target_pairs={{0,6},{1,7},{2,4},{3,5},{4,2},{5,3},{6,0},{7,1},{8,14},{9,15},{10,... | collective-permute-start | bytes 393224 | tf_op jit(solution)/shard_map/ppermute | solution.py:646
  494.5 12.2 %collective-permute-start.58 = (f32[1,2,2,64,128]{4,3,2,1,0:T(8,128)S(1)}, f32[1,2,2,64,128]{4,3,2,1,0:T(8,128)S(1)}, u32[]{:S(2)}, u32[]{:S(2)}) collective-permute-start(f32[1,2,2,64,128]{4,3,2,1,0:T(8,128)S(1)} %bitcast.149), channel_id=1, source_target_pairs={{0,14},{1,15},{2,12},{3,13},{4,10},{5,11},{6,8},{7,9},{8,6},{9,7},... | collective-permute-start | bytes 393224 | tf_op jit(solution)/shard_map/ppermute | solution.py:646
  495.6 25.5 %collective-permute-start.59 = (f32[1,2,2,64,128]{4,3,2,1,0:T(8,128)S(1)}, f32[1,2,2,64,128]{4,3,2,1,0:T(8,128)S(1)}, u32[]{:S(2)}, u32[]{:S(2)}) collective-permute-start(f32[1,2,2,64,128]{4,3,2,1,0:T(8,128)S(1)} %bitcast.145), channel_id=1, source_target_pairs={{0,15},{1,14},{2,13},{3,12},{4,11},{5,10},{6,9},{7,8},{8,7},{9,6},... | collective-permute-start | bytes 393224 | tf_op jit(solution)/shard_map/ppermute | solution.py:646
  497.4 30.9 %collective-permute-start.57 = (f32[1,2,2,64,128]{4,3,2,1,0:T(8,128)S(1)}, f32[1,2,2,64,128]{4,3,2,1,0:T(8,128)S(1)}, u32[]{:S(2)}, u32[]{:S(2)}) collective-permute-start(f32[1,2,2,64,128]{4,3,2,1,0:T(8,128)S(1)} %bitcast.141), channel_id=1, source_target_pairs={{0,13},{1,12},{2,15},{3,14},{4,9},{5,8},{6,11},{7,10},{8,5},{9,4},... | collective-permute-start | bytes 393224 | tf_op jit(solution)/shard_map/ppermute | solution.py:646
  497.4 32.1 %collective-permute-start.56 = (f32[1,2,2,64,128]{4,3,2,1,0:T(8,128)S(1)}, f32[1,2,2,64,128]{4,3,2,1,0:T(8,128)S(1)}, u32[]{:S(2)}, u32[]{:S(2)}) collective-permute-start(f32[1,2,2,64,128]{4,3,2,1,0:T(8,128)S(1)} %bitcast.137), channel_id=1, source_target_pairs={{0,12},{1,13},{2,14},{3,15},{4,8},{5,9},{6,10},{7,11},{8,4},{9,5},... | collective-permute-start | bytes 393224 | tf_op jit(solution)/shard_map/ppermute | solution.py:646
  498.6 33.1 %collective-permute-start.55 = (f32[1,2,2,64,128]{4,3,2,1,0:T(8,128)S(1)}, f32[1,2,2,64,128]{4,3,2,1,0:T(8,128)S(1)}, u32[]{:S(2)}, u32[]{:S(2)}) collective-permute-start(f32[1,2,2,64,128]{4,3,2,1,0:T(8,128)S(1)} %bitcast.133), channel_id=1, source_target_pairs={{0,11},{1,10},{2,9},{3,8},{4,15},{5,14},{6,13},{7,12},{8,3},{9,2},... | collective-permute-start | bytes 393224 | tf_op jit(solution)/shard_map/ppermute | solution.py:646
  506.7 30.7 %collective-permute-start.54 = (f32[1,2,2,64,128]{4,3,2,1,0:T(8,128)S(1)}, f32[1,2,2,64,128]{4,3,2,1,0:T(8,128)S(1)}, u32[]{:S(2)}, u32[]{:S(2)}) collective-permute-start(f32[1,2,2,64,128]{4,3,2,1,0:T(8,128)S(1)} %bitcast.129), channel_id=1, source_target_pairs={{0,10},{1,11},{2,8},{3,9},{4,14},{5,15},{6,12},{7,13},{8,2},{9,3},... | collective-permute-start | bytes 393224 | tf_op jit(solution)/shard_map/ppermute | solution.py:646
  521.1 18.7 %collective-permute-start.53 = (f32[1,2,2,64,128]{4,3,2,1,0:T(8,128)S(1)}, f32[1,2,2,64,128]{4,3,2,1,0:T(8,128)S(1)}, u32[]{:S(2)}, u32[]{:S(2)}) collective-permute-start(f32[1,2,2,64,128]{4,3,2,1,0:T(8,128)S(1)} %bitcast.125), channel_id=1, source_target_pairs={{0,9},{1,8},{2,11},{3,10},{4,13},{5,12},{6,15},{7,14},{8,1},{9,0},... | collective-permute-start | bytes 393224 | tf_op jit(solution)/shard_map/ppermute | solution.py:646
  528.3 13.8 %collective-permute-start.52 = (f32[1,2,2,64,128]{4,3,2,1,0:T(8,128)S(1)}, f32[1,2,2,64,128]{4,3,2,1,0:T(8,128)S(1)}, u32[]{:S(2)}, u32[]{:S(2)}) collective-permute-start(f32[1,2,2,64,128]{4,3,2,1,0:T(8,128)S(1)} %bitcast.121), channel_id=1, source_target_pairs={{0,8},{1,9},{2,10},{3,11},{4,12},{5,13},{6,14},{7,15},{8,0},{9,1},... | collective-permute-start | bytes 393224 | tf_op jit(solution)/shard_map/ppermute | solution.py:646
  529.6 12.5 %collective-permute-start.51 = (f32[1,2,2,64,128]{4,3,2,1,0:T(8,128)S(1)}, f32[1,2,2,64,128]{4,3,2,1,0:T(8,128)S(1)}, u32[]{:S(2)}, u32[]{:S(2)}) collective-permute-start(f32[1,2,2,64,128]{4,3,2,1,0:T(8,128)S(1)} %bitcast.117), channel_id=1, source_target_pairs={{0,7},{1,6},{2,5},{3,4},{4,3},{5,2},{6,1},{7,0},{8,15},{9,14},{10,... | collective-permute-start | bytes 393224 | tf_op jit(solution)/shard_map/ppermute | solution.py:646
  531.7 13.3 %collective-permute-start.50 = (f32[1,2,2,64,128]{4,3,2,1,0:T(8,128)S(1)}, f32[1,2,2,64,128]{4,3,2,1,0:T(8,128)S(1)}, u32[]{:S(2)}, u32[]{:S(2)}) collective-permute-start(f32[1,2,2,64,128]{4,3,2,1,0:T(8,128)S(1)} %bitcast.113), channel_id=1, source_target_pairs={{0,6},{1,7},{2,4},{3,5},{4,2},{5,3},{6,0},{7,1},{8,14},{9,15},{10,... | collective-permute-start | bytes 393224 | tf_op jit(solution)/shard_map/ppermute | solution.py:646
  537.4 15.9 %collective-permute-start.49 = (f32[1,2,2,64,128]{4,3,2,1,0:T(8,128)}, f32[1,2,2,64,128]{4,3,2,1,0:T(8,128)S(1)}, u32[]{:S(2)}, u32[]{:S(2)}) collective-permute-start(f32[1,2,2,64,128]{4,3,2,1,0:T(8,128)} %bitcast.63), channel_id=1, source_target_pairs={{0,5},{1,4},{2,7},{3,6},{4,1},{5,0},{6,3},{7,2},{8,13},{9,12},{10,... | collective-permute-start | bytes 393224 | tf_op jit(solution)/shard_map/ppermute | solution.py:646
  539.8 13.5 %collective-permute-start.48 = (f32[1,2,2,64,128]{4,3,2,1,0:T(8,128)}, f32[1,2,2,64,128]{4,3,2,1,0:T(8,128)S(1)}, u32[]{:S(2)}, u32[]{:S(2)}) collective-permute-start(f32[1,2,2,64,128]{4,3,2,1,0:T(8,128)} %bitcast.62), channel_id=1, source_target_pairs={{0,4},{1,5},{2,6},{3,7},{4,0},{5,1},{6,2},{7,3},{8,12},{9,13},{10,... | collective-permute-start | bytes 393224 | tf_op jit(solution)/shard_map/ppermute | solution.py:646
  542.1 11.2 %collective-permute-start.47 = (f32[1,2,2,64,128]{4,3,2,1,0:T(8,128)}, f32[1,2,2,64,128]{4,3,2,1,0:T(8,128)S(1)}, u32[]{:S(2)}, u32[]{:S(2)}) collective-permute-start(f32[1,2,2,64,128]{4,3,2,1,0:T(8,128)} %bitcast.61), channel_id=1, source_target_pairs={{0,3},{1,2},{2,1},{3,0},{4,7},{5,6},{6,5},{7,4},{8,11},{9,10},{10,... | collective-permute-start | bytes 393224 | tf_op jit(solution)/shard_map/ppermute | solution.py:646
  542.1 11.2 %collective-permute-start.46 = (f32[1,2,2,64,128]{4,3,2,1,0:T(8,128)}, f32[1,2,2,64,128]{4,3,2,1,0:T(8,128)S(1)}, u32[]{:S(2)}, u32[]{:S(2)}) collective-permute-start(f32[1,2,2,64,128]{4,3,2,1,0:T(8,128)} %bitcast.60), channel_id=1, source_target_pairs={{0,2},{1,3},{2,0},{3,1},{4,6},{5,7},{6,4},{7,5},{8,10},{9,11},{10,... | collective-permute-start | bytes 393224 | tf_op jit(solution)/shard_map/ppermute | solution.py:646
  (77 other events, 928.7 us)
where the time goes:
time: 575 us; the launch traced here: 571 us
  waiting for transfers between devices  221 us (38%)
  Pallas kernels  154 us (27%)
  starting transfers between devices  118 us (21%)
  blocking collectives  56 us (10%)
  local copies, waits for them, and re-layouts  20.6 us (4%)
    ppermute x60, waiting for transfers between devices, exchange(): arrived.append(lax.ppermute(sent[s:s + 1], 'mom', route))  188 us
    pallas_call x13, Pallas kernels, call(): pl.pallas_call(kernel, grid_spec=pltpu.PrefetchScalarGridSpec(num_scalar_...  154 us
    ppermute x60, starting transfers between devices, exchange(): arrived.append(lax.ppermute(sent[s:s + 1], 'mom', route))  100 us
    all_to_all x1, blocking collectives, exchange(): return lax.all_to_all(sent, 'mom', split_axis=0, concat_axis=0, tiled=True)  56 us
    all_to_all x3, waiting for transfers between devices, exchange(): return lax.all_to_all(sent, 'mom', split_axis=0, concat_axis=0, tiled=True)  33 us
    all_to_all x3, starting transfers between devices, exchange(): return lax.all_to_all(sent, 'mom', split_axis=0, concat_axis=0, tiled=True)  17.2 us
  transfers between devices with their start and end apart: 63, of which 28 were waited for; matrix products, arithmetic and copies ran while one was open for 2% of the time, Pallas kernels for 12%

commit v1 on v0

--- a/solution.py
+++ b/solution.py
@@ -31,7 +31,7 @@
     return lax.dot_general(a, b, (((1,), (1,)), ((), ())), preferred_element_type=F32)
 
 
-def call(kernel, flops, moved, args, grid, in_specs, out_specs, out_shape, scratch_shapes=(), scalars=(), aliases=None):
+def call(kernel, flops, moved, args, grid, in_specs, out_specs, out_shape, scratch_shapes=(), scalars=(), aliases=None, limit=VMEM_LIMIT):
     return pl.pallas_call(
         kernel,
         grid_spec=pltpu.PrefetchScalarGridSpec(
@@ -43,7 +43,7 @@
         ),
         out_shape=out_shape,
         input_output_aliases=aliases or {},
-        compiler_params=pltpu.CompilerParams(vmem_limit_bytes=VMEM_LIMIT),
+        compiler_params=pltpu.CompilerParams(vmem_limit_bytes=limit),
         cost_estimate=pl.CostEstimate(flops=flops, bytes_accessed=moved, transcendentals=0),
     )(*scalars, *args)
 
@@ -443,6 +443,7 @@
         + [pltpu.VMEM((angles * size, wide), BF16)] * 2
         + wholes,
         scalars=(flip,),
+        limit=44 << 20,
     )
 
 
@@ -579,6 +580,7 @@
         scratch_shapes=[pltpu.VMEM((size, channels), F32)] if len(backs) > 1 else [],
         scalars=(flip,),
         aliases=aliases,
+        limit=16 << 20,
     )
 
 

time: 575 us -> 582 us (1.012)
  local copies, waits for them, and re-layouts: 20.6 us -> 45.4 us
  waiting for transfers between devices: 221 us -> 211 us
  Pallas kernels: 154 us -> 146 us
    unnamed x126 -> x140, local copies, waits for them, and re-layouts: 9.09 us -> 35.3 us
    ppermute x60, waiting for transfers between devices: 188 us -> 178 us  [exchange(): arrived.append(lax.ppermute(sent[s:s + 1], 'mom', route))]
    pallas_call x13, Pallas kernels: 154 us -> 146 us  [call(): pl.pallas_call(kernel, grid_spec=pltpu.PrefetchScalarGridSpec(num_scalar_...]
  transfers between devices with their start and end apart: 63 -> 63, of which waited for: 28 -> 28; matrix products, arithmetic and copies ran while one was open for 2% -> 2% of each run, Pallas kernels for 12% -> 11%
where the time goes in v1:
time: 582 us; the launch traced here: 578 us
  waiting for transfers between devices  211 us (36%)
  Pallas kernels  146 us (25%)
  starting transfers between devices  118 us (20%)
  blocking collectives  55.5 us (10%)
  local copies, waits for them, and re-layouts  45.4 us (8%)
    ppermute x60, waiting for transfers between devices, exchange(): arrived.append(lax.ppermute(sent[s:s + 1], 'mom', route))  178 us
    pallas_call x13, Pallas kernels, call(): pl.pallas_call(kernel, grid_spec=pltpu.PrefetchScalarGridSpec(num_scalar_...  146 us
    ppermute x60, starting transfers between devices, exchange(): arrived.append(lax.ppermute(sent[s:s + 1], 'mom', route))  100 us
    all_to_all x1, blocking collectives, exchange(): return lax.all_to_all(sent, 'mom', split_axis=0, concat_axis=0, tiled=True)  55.5 us
    unnamed x140, local copies, waits for them, and re-layouts  35.3 us
    all_to_all x3, waiting for transfers between devices, exchange(): return lax.all_to_all(sent, 'mom', split_axis=0, concat_axis=0, tiled=True)  32.9 us
    all_to_all x3, starting transfers between devices, exchange(): return lax.all_to_all(sent, 'mom', split_axis=0, concat_axis=0, tiled=True)  17.5 us
  transfers between devices with their start and end apart: 63, of which 28 were waited for; matrix products, arithmetic and copies ran while one was open for 2% of the time, Pallas kernels for 11%

profile of v1, /device:TPU:9, one launch (start us, length us, event | category | flops | bytes accessed | tf_op | source)
XLA Modules:
  0.0 578.0 jit_solution(18149633274938046678)
XLA Ops:
  1.8 18.6 %shard_map.131 = (f32[16,2,2,2,32,128]{5,4,3,2,1,0:T(8,128)}, bf16[1024,2048]{1,0:T(8,128)(2,1)}, bf16[1024,2048]{1,0:T(8,128)(2,1)}) custom-call(s32[2]{0:T(128)} %pad_add_fusion.1.flip_ref, f32[8,128,1024]{2,1,0:T(8,128)} %source_ref.7, f32[2,4,128,128]{3,2,1,0:T(8,128)} %refs_17_.3, s32[2,1024]{1,0:T(2,128)} %refs_0_.1, s32[2,1024]{1,0:T(2,128)} %refs_1_.2, ...), custom_call_target="tpu_custom_call" | custom-call | flops 7247757312 | bytes 12582912 | tf_op jit(solution)/shard_map/pallas_call | solution.py:35
  20.4 13.5 %shard_map.132 = f32[16,2,2,2,32,128]{5,4,3,2,1,0:T(8,128)} custom-call(s32[2]{0:T(128)} %pad_add_fusion.flip_ref, f32[8,128,1024]{2,1,0:T(8,128)} %source_ref.7, f32[2,4,128,128]{3,2,1,0:T(8,128)} %refs_17_.3, bf16[1024,2048]{1,0:T(8,128)(2,1)} %get-tuple-element.7.high_ref.refs_18_, bf16[1024,2048]{1,0:T(8,128)(2,1)} %get-tuple-element.8.low_ref.refs_19_), custom_call_target="tpu_custom_call" | custom-call | flops 7247757312 | bytes 12582912 | tf_op jit(solution)/shard_map/pallas_call | solution.py:35
  34.0 6.7 %all-to-all-start = ((f32[16,2,2,64,128]{4,3,2,1,0:T(8,128)}), f32[16,2,2,64,128]{4,3,2,1,0:T(8,128)S(1)}, u32[]{:S(2)}, u32[]{:S(2)}) async-start(f32[16,2,2,64,128]{4,3,2,1,0:T(8,128)} %bitcast.89), calls=%async_computation | async-start | bytes 4194304 | tf_op jit(solution)/shard_map/all_to_all | solution.py:644
  45.6 8.3 %shard_map.133 = (bf16[1024,2048]{1,0:T(8,128)(2,1)}, bf16[1024,2048]{1,0:T(8,128)(2,1)}) custom-call(s32[2,1024]{1,0:T(2,128)} %reshape.123.refs_0_, s32[2,1024]{1,0:T(2,128)} %reshape.125.refs_1_, f32[2,4,1024]{2,1,0:T(4,128)} %reshape.127.refs_2_, f32[2,4,1024]{2,1,0:T(4,128)} %reshape.129.refs_3_), custom_call_target="tpu_custom_call" | custom-call | flops 20971520 | bytes 8388608 | tf_op jit(solution)/shard_map/pallas_call | solution.py:35
  53.9 32.9 %all-to-all-done.refs_0_ = f32[16,2,2,64,128]{4,3,2,1,0:T(8,128)S(1)} async-done(((f32[16,2,2,64,128]{4,3,2,1,0:T(8,128)}), f32[16,2,2,64,128]{4,3,2,1,0:T(8,128)S(1)}, u32[]{:S(2)}, u32[]{:S(2)}) %all-to-all-start) | async-done | bytes 2097184 | tf_op jit(solution)/shard_map/all_to_all | solution.py:644
  88.1 14.4 %shard_map.135 = f32[16,2,2,2,32,128]{5,4,3,2,1,0:T(8,128)} custom-call(s32[2]{0:T(128)} %pad_add_fusion.flip_ref, f32[16,2,2,64,128]{4,3,2,1,0:T(8,128)} %copy-done.38, f32[2,4,128,128]{3,2,1,0:T(8,128)} %refs_32_.1, f32[1024,4]{1,0:T(8,128)} %copy.29.refs_2_.refs_3_, bf16[1024,2048]{1,0:T(8,128)(2,1)} %get-tuple-element.10.refs_18_.refs_3_.refs_4_.refs_34_, ...), custom_call_target="tpu_custom_call" | custom-call | flops 7247757312 | bytes 10485760 | tf_op jit(solution)/shard_map/pallas_call | solution.py:35
  102.5 6.1 %all-to-all-start.1 = ((f32[16,2,2,64,128]{4,3,2,1,0:T(8,128)}), f32[16,2,2,64,128]{4,3,2,1,0:T(8,128)S(1)}, u32[]{:S(2)}, u32[]{:S(2)}) async-start(f32[16,2,2,64,128]{4,3,2,1,0:T(8,128)} %bitcast.88), calls=%async_computation.1 | async-start | bytes 4194304 | tf_op jit(solution)/shard_map/all_to_all | solution.py:644
  114.5 7.4 %collective-permute-start.10 = (f32[1,2,2,64,128]{4,3,2,1,0:T(8,128)S(1)}, f32[1,2,2,64,128]{4,3,2,1,0:T(8,128)S(1)}, u32[]{:S(2)}, u32[]{:S(2)}) collective-permute-start(f32[1,2,2,64,128]{4,3,2,1,0:T(8,128)S(1)} %bitcast.130), channel_id=1, source_target_pairs={{0,11},{1,10},{2,9},{3,8},{4,15},{5,14},{6,13},{7,12},{8,3},{9,2},... | collective-permute-start | bytes 393224 | tf_op jit(solution)/shard_map/ppermute | solution.py:648
  121.9 51.5 %collective-permute-done.13.refs_14_ = f32[1,2,2,64,128]{4,3,2,1,0:T(8,128)S(1)} collective-permute-done((f32[1,2,2,64,128]{4,3,2,1,0:T(8,128)S(1)}, f32[1,2,2,64,128]{4,3,2,1,0:T(8,128)S(1)}, u32[]{:S(2)}, u32[]{:S(2)}) %collective-permute-start.13) | collective-permute-done | bytes 131104 | tf_op jit(solution)/shard_map/ppermute | solution.py:648
  173.5 3.7 collective-permute-done.14.refs_15_
  177.5 7.1 %collective-permute-done.12.refs_13_ = f32[1,2,2,64,128]{4,3,2,1,0:T(8,128)S(1)} collective-permute-done((f32[1,2,2,64,128]{4,3,2,1,0:T(8,128)S(1)}, f32[1,2,2,64,128]{4,3,2,1,0:T(8,128)S(1)}, u32[]{:S(2)}, u32[]{:S(2)}) %collective-permute-start.12) | collective-permute-done | bytes 131104 | tf_op jit(solution)/shard_map/ppermute | solution.py:648
  186.9 3.4 collective-permute-done.10.refs_11_
  190.3 5.0 collective-permute-start.5
  195.2 3.4 collective-permute-start.4
  205.9 2.8 collective-permute-done.3.refs_4_
  208.7 14.6 %shard_map.134 = f32[16,2,2,2,32,128]{5,4,3,2,1,0:T(8,128)} custom-call(s32[2]{0:T(128)} %pad_add_fusion.1.flip_ref, f32[16,2,2,64,128]{4,3,2,1,0:T(8,128)} %bitcast.90, f32[1,2,2,64,128]{4,3,2,1,0:T(8,128)} %collective-permute-done.refs_1_, f32[1,2,2,64,128]{4,3,2,1,0:T(8,128)} %collective-permute-done.1.refs_2_, ...), custom_call_target="tpu_custom_call" | custom-call | flops 7247757312 | bytes 10485760 | tf_op jit(solution)/shard_map/pallas_call | solution.py:35
  229.3 8.3 %collective-permute-start.25 = (f32[1,2,2,64,128]{4,3,2,1,0:T(8,128)S(1)}, f32[1,2,2,64,128]{4,3,2,1,0:T(8,128)S(1)}, u32[]{:S(2)}, u32[]{:S(2)}) collective-permute-start(f32[1,2,2,64,128]{4,3,2,1,0:T(8,128)S(1)} %bitcast.131), channel_id=1, source_target_pairs={{0,11},{1,10},{2,9},{3,8},{4,15},{5,14},{6,13},{7,12},{8,3},{9,2},... | collective-permute-start | bytes 393224 | tf_op jit(solution)/shard_map/ppermute | solution.py:648
  237.6 14.2 %collective-permute-done.29.refs_15_ = f32[1,2,2,64,128]{4,3,2,1,0:T(8,128)S(1)} collective-permute-done((f32[1,2,2,64,128]{4,3,2,1,0:T(8,128)S(1)}, f32[1,2,2,64,128]{4,3,2,1,0:T(8,128)S(1)}, u32[]{:S(2)}, u32[]{:S(2)}) %collective-permute-start.29) | collective-permute-done | bytes 131104 | tf_op jit(solution)/shard_map/ppermute | solution.py:648
  251.8 7.2 %collective-permute-done.27.refs_13_ = f32[1,2,2,64,128]{4,3,2,1,0:T(8,128)S(1)} collective-permute-done((f32[1,2,2,64,128]{4,3,2,1,0:T(8,128)S(1)}, f32[1,2,2,64,128]{4,3,2,1,0:T(8,128)S(1)}, u32[]{:S(2)}, u32[]{:S(2)}) %collective-permute-start.27) | collective-permute-done | bytes 131104 | tf_op jit(solution)/shard_map/ppermute | solution.py:648
  262.5 5.6 collective-permute-start.20
  268.1 2.4 collective-permute-start.19
  276.3 3.0 collective-permute-start.15
  293.6 14.3 %shard_map.136 = f32[16,2,2,2,32,128]{5,4,3,2,1,0:T(8,128)S(1)} custom-call(s32[2]{0:T(128)S(1)} %copy-done.8, f32[16,2,2,64,128]{4,3,2,1,0:T(8,128)S(1)} %bitcast.85, f32[1,2,2,64,128]{4,3,2,1,0:T(8,128)S(1)} %copy-done.36, f32[1,2,2,64,128]{4,3,2,1,0:T(8,128)S(1)} %copy-done.33, f32[1,2,2,64,128]{4,3,2,1,0:T(8,128)S(1)} %copy-done.30, ...), custom_call_target="tpu_custom_call" | custom-call | flops 9663676416 | bytes 12582912 | tf_op jit(solution)/shard_map/pallas_call | solution.py:35
  308.0 55.5 %all_to_all.20.refs_1_ = f32[16,2,2,64,128]{4,3,2,1,0:T(8,128)} all-to-all(f32[16,2,2,64,128]{4,3,2,1,0:T(8,128)S(1)} %bitcast.83), channel_id=1, replica_groups=mesh['energy'=2,'mom'=16] {'mom'}, dimensions={0} | all-to-all | bytes 4194304 | tf_op jit(solution)/shard_map/all_to_all | solution.py:644
  363.5 15.0 %shard_map.137.sent_ref = f32[16,2,2,2,32,128]{5,4,3,2,1,0:T(8,128)} custom-call(s32[2]{0:T(128)} %pad_add_fusion.flip_ref, f32[16,2,2,64,128]{4,3,2,1,0:T(8,128)} %copy-done.38, f32[16,2,2,64,128]{4,3,2,1,0:T(8,128)} %all_to_all.20.refs_1_, f32[2,4,128,128]{3,2,1,0:T(8,128)} %refs_32_.1, f32[1024,4]{1,0:T(8,128)} %copy.29.refs_2_.refs_3_, ...), custom_call_target="tpu_custom_call" | custom-call | flops 7247757312 | bytes 12582912 | tf_op jit(solution)/shard_map/pallas_call | solution.py:35
  378.5 4.7 all-to-all-start.3
  393.0 14.3 %shard_map.138 = f32[16,2,2,2,32,128]{5,4,3,2,1,0:T(8,128)S(1)} custom-call(s32[2]{0:T(128)S(1)} %copy-done.6, f32[16,2,2,64,128]{4,3,2,1,0:T(8,128)S(1)} %bitcast.86, f32[1,2,2,64,128]{4,3,2,1,0:T(8,128)S(1)} %copy-done.37, f32[1,2,2,64,128]{4,3,2,1,0:T(8,128)S(1)} %copy-done.34, f32[1,2,2,64,128]{4,3,2,1,0:T(8,128)S(1)} %copy-done.31, ...), custom_call_target="tpu_custom_call" | custom-call | flops 9663676416 | bytes 12582912 | tf_op jit(solution)/shard_map/pallas_call | solution.py:35
  413.0 7.3 %collective-permute-start.40 = (f32[1,2,2,64,128]{4,3,2,1,0:T(8,128)S(1)}, f32[1,2,2,64,128]{4,3,2,1,0:T(8,128)S(1)}, u32[]{:S(2)}, u32[]{:S(2)}) collective-permute-start(f32[1,2,2,64,128]{4,3,2,1,0:T(8,128)S(1)} %bitcast.132), channel_id=1, source_target_pairs={{0,11},{1,10},{2,9},{3,8},{4,15},{5,14},{6,13},{7,12},{8,3},{9,2},... | collective-permute-start | bytes 393224 | tf_op jit(solution)/shard_map/ppermute | solution.py:648
  420.3 27.7 %collective-permute-done.43.refs_30_ = f32[1,2,2,64,128]{4,3,2,1,0:T(8,128)S(1)} collective-permute-done((f32[1,2,2,64,128]{4,3,2,1,0:T(8,128)S(1)}, f32[1,2,2,64,128]{4,3,2,1,0:T(8,128)S(1)}, u32[]{:S(2)}, u32[]{:S(2)}) %collective-permute-start.43) | collective-permute-done | bytes 131104 | tf_op jit(solution)/shard_map/ppermute | solution.py:648
  448.0 3.7 collective-permute-done.44.refs_31_
  452.0 7.1 %collective-permute-done.42.refs_29_ = f32[1,2,2,64,128]{4,3,2,1,0:T(8,128)S(1)} collective-permute-done((f32[1,2,2,64,128]{4,3,2,1,0:T(8,128)S(1)}, f32[1,2,2,64,128]{4,3,2,1,0:T(8,128)S(1)}, u32[]{:S(2)}, u32[]{:S(2)}) %collective-permute-start.42) | collective-permute-done | bytes 131104 | tf_op jit(solution)/shard_map/ppermute | solution.py:648
  461.4 3.4 collective-permute-done.40.refs_27_
  464.8 5.0 collective-permute-start.35
  469.8 3.4 collective-permute-start.34
  478.0 2.4 collective-permute-done.34.refs_21_
  480.4 2.8 collective-permute-done.33.refs_20_
  484.0 15.1 %shard_map.139.sent_ref = f32[16,2,2,2,32,128]{5,4,3,2,1,0:T(8,128)} custom-call(s32[2]{0:T(128)} %pad_add_fusion.1.flip_ref, f32[16,2,2,64,128]{4,3,2,1,0:T(8,128)} %bitcast.91, f32[1,2,2,64,128]{4,3,2,1,0:T(8,128)} %collective-permute-done.refs_1_, f32[1,2,2,64,128]{4,3,2,1,0:T(8,128)} %collective-permute-done.1.refs_2_, ...), custom_call_target="tpu_custom_call" | custom-call | flops 7247757312 | bytes 12582912 | tf_op jit(solution)/shard_map/pallas_call | solution.py:35
  499.1 2.5 fusion
  505.7 8.1 %collective-permute-start.55 = (f32[1,2,2,64,128]{4,3,2,1,0:T(8,128)S(1)}, f32[1,2,2,64,128]{4,3,2,1,0:T(8,128)S(1)}, u32[]{:S(2)}, u32[]{:S(2)}) collective-permute-start(f32[1,2,2,64,128]{4,3,2,1,0:T(8,128)S(1)} %bitcast.133), channel_id=1, source_target_pairs={{0,11},{1,10},{2,9},{3,8},{4,15},{5,14},{6,13},{7,12},{8,3},{9,2},... | collective-permute-start | bytes 393224 | tf_op jit(solution)/shard_map/ppermute | solution.py:648
  513.8 14.4 %collective-permute-done.59.refs_15_ = f32[1,2,2,64,128]{4,3,2,1,0:T(8,128)S(1)} collective-permute-done((f32[1,2,2,64,128]{4,3,2,1,0:T(8,128)S(1)}, f32[1,2,2,64,128]{4,3,2,1,0:T(8,128)S(1)}, u32[]{:S(2)}, u32[]{:S(2)}) %collective-permute-start.59) | collective-permute-done | bytes 131104 | tf_op jit(solution)/shard_map/ppermute | solution.py:648
  528.2 7.1 %collective-permute-done.57.refs_13_ = f32[1,2,2,64,128]{4,3,2,1,0:T(8,128)S(1)} collective-permute-done((f32[1,2,2,64,128]{4,3,2,1,0:T(8,128)S(1)}, f32[1,2,2,64,128]{4,3,2,1,0:T(8,128)S(1)}, u32[]{:S(2)}, u32[]{:S(2)}) %collective-permute-start.57) | collective-permute-done | bytes 131104 | tf_op jit(solution)/shard_map/ppermute | solution.py:648
  538.8 5.7 collective-permute-start.50
  544.5 2.5 collective-permute-start.49
  552.1 3.0 collective-permute-start.45
  555.1 5.3 shard_map.142.refs_0_
  562.6 3.0 shard_map.140.refs_1_
  565.7 5.4 shard_map.143
  573.2 4.8 shard_map.141
  (254 shorter events, 93.2 us)
Async XLA Ops:
  34.0 52.8 %all-to-all-start = ((f32[16,2,2,64,128]{4,3,2,1,0:T(8,128)}), f32[16,2,2,64,128]{4,3,2,1,0:T(8,128)S(1)}, u32[]{:S(2)}, u32[]{:S(2)}) async-start(f32[16,2,2,64,128]{4,3,2,1,0:T(8,128)} %bitcast.89), calls=%async_computation | async-start | bytes 4194304 | tf_op jit(solution)/shard_map/all_to_all | solution.py:644
  102.5 181.4 %all-to-all-start.1 = ((f32[16,2,2,64,128]{4,3,2,1,0:T(8,128)}), f32[16,2,2,64,128]{4,3,2,1,0:T(8,128)S(1)}, u32[]{:S(2)}, u32[]{:S(2)}) async-start(f32[16,2,2,64,128]{4,3,2,1,0:T(8,128)} %bitcast.88), calls=%async_computation.1 | async-start | bytes 4194304 | tf_op jit(solution)/shard_map/all_to_all | solution.py:644
  110.3 63.1 %collective-permute-start.13 = (f32[1,2,2,64,128]{4,3,2,1,0:T(8,128)S(1)}, f32[1,2,2,64,128]{4,3,2,1,0:T(8,128)S(1)}, u32[]{:S(2)}, u32[]{:S(2)}) collective-permute-start(f32[1,2,2,64,128]{4,3,2,1,0:T(8,128)S(1)} %bitcast.146), channel_id=1, source_target_pairs={{0,14},{1,15},{2,12},{3,13},{4,10},{5,11},{6,8},{7,9},{8,6},{9,7},... | collective-permute-start | bytes 393224 | tf_op jit(solution)/shard_map/ppermute | solution.py:648
  112.5 64.7 %collective-permute-start.14 = (f32[1,2,2,64,128]{4,3,2,1,0:T(8,128)S(1)}, f32[1,2,2,64,128]{4,3,2,1,0:T(8,128)S(1)}, u32[]{:S(2)}, u32[]{:S(2)}) collective-permute-start(f32[1,2,2,64,128]{4,3,2,1,0:T(8,128)S(1)} %bitcast.142), channel_id=1, source_target_pairs={{0,15},{1,14},{2,13},{3,12},{4,11},{5,10},{6,9},{7,8},{8,7},{9,6},... | collective-permute-start | bytes 393224 | tf_op jit(solution)/shard_map/ppermute | solution.py:648
  113.3 71.3 %collective-permute-start.12 = (f32[1,2,2,64,128]{4,3,2,1,0:T(8,128)S(1)}, f32[1,2,2,64,128]{4,3,2,1,0:T(8,128)S(1)}, u32[]{:S(2)}, u32[]{:S(2)}) collective-permute-start(f32[1,2,2,64,128]{4,3,2,1,0:T(8,128)S(1)} %bitcast.138), channel_id=1, source_target_pairs={{0,13},{1,12},{2,15},{3,14},{4,9},{5,8},{6,11},{7,10},{8,5},{9,4},... | collective-permute-start | bytes 393224 | tf_op jit(solution)/shard_map/ppermute | solution.py:648
  114.2 72.3 %collective-permute-start.11 = (f32[1,2,2,64,128]{4,3,2,1,0:T(8,128)S(1)}, f32[1,2,2,64,128]{4,3,2,1,0:T(8,128)S(1)}, u32[]{:S(2)}, u32[]{:S(2)}) collective-permute-start(f32[1,2,2,64,128]{4,3,2,1,0:T(8,128)S(1)} %bitcast.134), channel_id=1, source_target_pairs={{0,12},{1,13},{2,14},{3,15},{4,8},{5,9},{6,10},{7,11},{8,4},{9,5},... | collective-permute-start | bytes 393224 | tf_op jit(solution)/shard_map/ppermute | solution.py:648
  114.5 75.8 %collective-permute-start.10 = (f32[1,2,2,64,128]{4,3,2,1,0:T(8,128)S(1)}, f32[1,2,2,64,128]{4,3,2,1,0:T(8,128)S(1)}, u32[]{:S(2)}, u32[]{:S(2)}) collective-permute-start(f32[1,2,2,64,128]{4,3,2,1,0:T(8,128)S(1)} %bitcast.130), channel_id=1, source_target_pairs={{0,11},{1,10},{2,9},{3,8},{4,15},{5,14},{6,13},{7,12},{8,3},{9,2},... | collective-permute-start | bytes 393224 | tf_op jit(solution)/shard_map/ppermute | solution.py:648
  173.5 21.7 %collective-permute-start.9 = (f32[1,2,2,64,128]{4,3,2,1,0:T(8,128)S(1)}, f32[1,2,2,64,128]{4,3,2,1,0:T(8,128)S(1)}, u32[]{:S(2)}, u32[]{:S(2)}) collective-permute-start(f32[1,2,2,64,128]{4,3,2,1,0:T(8,128)S(1)} %bitcast.126), channel_id=1, source_target_pairs={{0,10},{1,11},{2,8},{3,9},{4,14},{5,15},{6,12},{7,13},{8,2},{9,3},... | collective-permute-start | bytes 393224 | tf_op jit(solution)/shard_map/ppermute | solution.py:648
  177.1 21.5 %collective-permute-start.8 = (f32[1,2,2,64,128]{4,3,2,1,0:T(8,128)S(1)}, f32[1,2,2,64,128]{4,3,2,1,0:T(8,128)S(1)}, u32[]{:S(2)}, u32[]{:S(2)}) collective-permute-start(f32[1,2,2,64,128]{4,3,2,1,0:T(8,128)S(1)} %bitcast.122), channel_id=1, source_target_pairs={{0,9},{1,8},{2,11},{3,10},{4,13},{5,12},{6,15},{7,14},{8,1},{9,0},... | collective-permute-start | bytes 393224 | tf_op jit(solution)/shard_map/ppermute | solution.py:648
  184.6 15.3 %collective-permute-start.7 = (f32[1,2,2,64,128]{4,3,2,1,0:T(8,128)S(1)}, f32[1,2,2,64,128]{4,3,2,1,0:T(8,128)S(1)}, u32[]{:S(2)}, u32[]{:S(2)}) collective-permute-start(f32[1,2,2,64,128]{4,3,2,1,0:T(8,128)S(1)} %bitcast.118), channel_id=1, source_target_pairs={{0,8},{1,9},{2,10},{3,11},{4,12},{5,13},{6,14},{7,15},{8,0},{9,1},... | collective-permute-start | bytes 393224 | tf_op jit(solution)/shard_map/ppermute | solution.py:648
  186.6 14.3 %collective-permute-start.6 = (f32[1,2,2,64,128]{4,3,2,1,0:T(8,128)S(1)}, f32[1,2,2,64,128]{4,3,2,1,0:T(8,128)S(1)}, u32[]{:S(2)}, u32[]{:S(2)}) collective-permute-start(f32[1,2,2,64,128]{4,3,2,1,0:T(8,128)S(1)} %bitcast.114), channel_id=1, source_target_pairs={{0,7},{1,6},{2,5},{3,4},{4,3},{5,2},{6,1},{7,0},{8,15},{9,14},{10,... | collective-permute-start | bytes 393224 | tf_op jit(solution)/shard_map/ppermute | solution.py:648
  190.3 12.8 %collective-permute-start.5 = (f32[1,2,2,64,128]{4,3,2,1,0:T(8,128)S(1)}, f32[1,2,2,64,128]{4,3,2,1,0:T(8,128)S(1)}, u32[]{:S(2)}, u32[]{:S(2)}) collective-permute-start(f32[1,2,2,64,128]{4,3,2,1,0:T(8,128)S(1)} %bitcast.110), channel_id=1, source_target_pairs={{0,6},{1,7},{2,4},{3,5},{4,2},{5,3},{6,0},{7,1},{8,14},{9,15},{10,... | collective-permute-start | bytes 393224 | tf_op jit(solution)/shard_map/ppermute | solution.py:648
  225.1 12.5 %collective-permute-start.28 = (f32[1,2,2,64,128]{4,3,2,1,0:T(8,128)S(1)}, f32[1,2,2,64,128]{4,3,2,1,0:T(8,128)S(1)}, u32[]{:S(2)}, u32[]{:S(2)}) collective-permute-start(f32[1,2,2,64,128]{4,3,2,1,0:T(8,128)S(1)} %bitcast.147), channel_id=1, source_target_pairs={{0,14},{1,15},{2,12},{3,13},{4,10},{5,11},{6,8},{7,9},{8,6},{9,7},... | collective-permute-start | bytes 393224 | tf_op jit(solution)/shard_map/ppermute | solution.py:648
  226.5 25.4 %collective-permute-start.29 = (f32[1,2,2,64,128]{4,3,2,1,0:T(8,128)S(1)}, f32[1,2,2,64,128]{4,3,2,1,0:T(8,128)S(1)}, u32[]{:S(2)}, u32[]{:S(2)}) collective-permute-start(f32[1,2,2,64,128]{4,3,2,1,0:T(8,128)S(1)} %bitcast.143), channel_id=1, source_target_pairs={{0,15},{1,14},{2,13},{3,12},{4,11},{5,10},{6,9},{7,8},{8,7},{9,6},... | collective-permute-start | bytes 393224 | tf_op jit(solution)/shard_map/ppermute | solution.py:648
  228.1 30.9 %collective-permute-start.27 = (f32[1,2,2,64,128]{4,3,2,1,0:T(8,128)S(1)}, f32[1,2,2,64,128]{4,3,2,1,0:T(8,128)S(1)}, u32[]{:S(2)}, u32[]{:S(2)}) collective-permute-start(f32[1,2,2,64,128]{4,3,2,1,0:T(8,128)S(1)} %bitcast.139), channel_id=1, source_target_pairs={{0,13},{1,12},{2,15},{3,14},{4,9},{5,8},{6,11},{7,10},{8,5},{9,4},... | collective-permute-start | bytes 393224 | tf_op jit(solution)/shard_map/ppermute | solution.py:648
  228.2 32.1 %collective-permute-start.26 = (f32[1,2,2,64,128]{4,3,2,1,0:T(8,128)S(1)}, f32[1,2,2,64,128]{4,3,2,1,0:T(8,128)S(1)}, u32[]{:S(2)}, u32[]{:S(2)}) collective-permute-start(f32[1,2,2,64,128]{4,3,2,1,0:T(8,128)S(1)} %bitcast.135), channel_id=1, source_target_pairs={{0,12},{1,13},{2,14},{3,15},{4,8},{5,9},{6,10},{7,11},{8,4},{9,5},... | collective-permute-start | bytes 393224 | tf_op jit(solution)/shard_map/ppermute | solution.py:648
  229.3 33.2 %collective-permute-start.25 = (f32[1,2,2,64,128]{4,3,2,1,0:T(8,128)S(1)}, f32[1,2,2,64,128]{4,3,2,1,0:T(8,128)S(1)}, u32[]{:S(2)}, u32[]{:S(2)}) collective-permute-start(f32[1,2,2,64,128]{4,3,2,1,0:T(8,128)S(1)} %bitcast.131), channel_id=1, source_target_pairs={{0,11},{1,10},{2,9},{3,8},{4,15},{5,14},{6,13},{7,12},{8,3},{9,2},... | collective-permute-start | bytes 393224 | tf_op jit(solution)/shard_map/ppermute | solution.py:648
  237.6 30.5 %collective-permute-start.24 = (f32[1,2,2,64,128]{4,3,2,1,0:T(8,128)S(1)}, f32[1,2,2,64,128]{4,3,2,1,0:T(8,128)S(1)}, u32[]{:S(2)}, u32[]{:S(2)}) collective-permute-start(f32[1,2,2,64,128]{4,3,2,1,0:T(8,128)S(1)} %bitcast.127), channel_id=1, source_target_pairs={{0,10},{1,11},{2,8},{3,9},{4,14},{5,15},{6,12},{7,13},{8,2},{9,3},... | collective-permute-start | bytes 393224 | tf_op jit(solution)/shard_map/ppermute | solution.py:648
  251.8 18.7 %collective-permute-start.23 = (f32[1,2,2,64,128]{4,3,2,1,0:T(8,128)S(1)}, f32[1,2,2,64,128]{4,3,2,1,0:T(8,128)S(1)}, u32[]{:S(2)}, u32[]{:S(2)}) collective-permute-start(f32[1,2,2,64,128]{4,3,2,1,0:T(8,128)S(1)} %bitcast.123), channel_id=1, source_target_pairs={{0,9},{1,8},{2,11},{3,10},{4,13},{5,12},{6,15},{7,14},{8,1},{9,0},... | collective-permute-start | bytes 393224 | tf_op jit(solution)/shard_map/ppermute | solution.py:648
  259.0 14.5 %collective-permute-start.22 = (f32[1,2,2,64,128]{4,3,2,1,0:T(8,128)S(1)}, f32[1,2,2,64,128]{4,3,2,1,0:T(8,128)S(1)}, u32[]{:S(2)}, u32[]{:S(2)}) collective-permute-start(f32[1,2,2,64,128]{4,3,2,1,0:T(8,128)S(1)} %bitcast.119), channel_id=1, source_target_pairs={{0,8},{1,9},{2,10},{3,11},{4,12},{5,13},{6,14},{7,15},{8,0},{9,1},... | collective-permute-start | bytes 393224 | tf_op jit(solution)/shard_map/ppermute | solution.py:648
  260.3 13.8 %collective-permute-start.21 = (f32[1,2,2,64,128]{4,3,2,1,0:T(8,128)S(1)}, f32[1,2,2,64,128]{4,3,2,1,0:T(8,128)S(1)}, u32[]{:S(2)}, u32[]{:S(2)}) collective-permute-start(f32[1,2,2,64,128]{4,3,2,1,0:T(8,128)S(1)} %bitcast.115), channel_id=1, source_target_pairs={{0,7},{1,6},{2,5},{3,4},{4,3},{5,2},{6,1},{7,0},{8,15},{9,14},{10,... | collective-permute-start | bytes 393224 | tf_op jit(solution)/shard_map/ppermute | solution.py:648
  262.5 13.2 %collective-permute-start.20 = (f32[1,2,2,64,128]{4,3,2,1,0:T(8,128)S(1)}, f32[1,2,2,64,128]{4,3,2,1,0:T(8,128)S(1)}, u32[]{:S(2)}, u32[]{:S(2)}) collective-permute-start(f32[1,2,2,64,128]{4,3,2,1,0:T(8,128)S(1)} %bitcast.111), channel_id=1, source_target_pairs={{0,6},{1,7},{2,4},{3,5},{4,2},{5,3},{6,0},{7,1},{8,14},{9,15},{10,... | collective-permute-start | bytes 393224 | tf_op jit(solution)/shard_map/ppermute | solution.py:648
  268.1 11.2 %collective-permute-start.19 = (f32[1,2,2,64,128]{4,3,2,1,0:T(8,128)S(1)}, f32[1,2,2,64,128]{4,3,2,1,0:T(8,128)S(1)}, u32[]{:S(2)}, u32[]{:S(2)}) collective-permute-start(f32[1,2,2,64,128]{4,3,2,1,0:T(8,128)S(1)} %bitcast.108), channel_id=1, source_target_pairs={{0,5},{1,4},{2,7},{3,6},{4,1},{5,0},{6,3},{7,2},{8,13},{9,12},{10,... | collective-permute-start | bytes 393224 | tf_op jit(solution)/shard_map/ppermute | solution.py:648
  378.5 192.5 %all-to-all-start.3 = ((f32[16,2,2,64,128]{4,3,2,1,0:T(8,128)}), f32[16,2,2,64,128]{4,3,2,1,0:T(8,128)}, u32[]{:S(2)}, u32[]{:S(2)}) async-start(f32[16,2,2,64,128]{4,3,2,1,0:T(8,128)} %bitcast.87), calls=%async_computation.3 | async-start | bytes 4194304 | tf_op jit(solution)/shard_map/all_to_all | solution.py:644
  408.8 39.2 %collective-permute-start.43 = (f32[1,2,2,64,128]{4,3,2,1,0:T(8,128)S(1)}, f32[1,2,2,64,128]{4,3,2,1,0:T(8,128)S(1)}, u32[]{:S(2)}, u32[]{:S(2)}) collective-permute-start(f32[1,2,2,64,128]{4,3,2,1,0:T(8,128)S(1)} %bitcast.148), channel_id=1, source_target_pairs={{0,14},{1,15},{2,12},{3,13},{4,10},{5,11},{6,8},{7,9},{8,6},{9,7},... | collective-permute-start | bytes 393224 | tf_op jit(solution)/shard_map/ppermute | solution.py:648
  410.8 40.9 %collective-permute-start.44 = (f32[1,2,2,64,128]{4,3,2,1,0:T(8,128)S(1)}, f32[1,2,2,64,128]{4,3,2,1,0:T(8,128)S(1)}, u32[]{:S(2)}, u32[]{:S(2)}) collective-permute-start(f32[1,2,2,64,128]{4,3,2,1,0:T(8,128)S(1)} %bitcast.144), channel_id=1, source_target_pairs={{0,15},{1,14},{2,13},{3,12},{4,11},{5,10},{6,9},{7,8},{8,7},{9,6},... | collective-permute-start | bytes 393224 | tf_op jit(solution)/shard_map/ppermute | solution.py:648
  411.7 47.5 %collective-permute-start.42 = (f32[1,2,2,64,128]{4,3,2,1,0:T(8,128)S(1)}, f32[1,2,2,64,128]{4,3,2,1,0:T(8,128)S(1)}, u32[]{:S(2)}, u32[]{:S(2)}) collective-permute-start(f32[1,2,2,64,128]{4,3,2,1,0:T(8,128)S(1)} %bitcast.140), channel_id=1, source_target_pairs={{0,13},{1,12},{2,15},{3,14},{4,9},{5,8},{6,11},{7,10},{8,5},{9,4},... | collective-permute-start | bytes 393224 | tf_op jit(solution)/shard_map/ppermute | solution.py:648
  412.6 48.5 %collective-permute-start.41 = (f32[1,2,2,64,128]{4,3,2,1,0:T(8,128)S(1)}, f32[1,2,2,64,128]{4,3,2,1,0:T(8,128)S(1)}, u32[]{:S(2)}, u32[]{:S(2)}) collective-permute-start(f32[1,2,2,64,128]{4,3,2,1,0:T(8,128)S(1)} %bitcast.136), channel_id=1, source_target_pairs={{0,12},{1,13},{2,14},{3,15},{4,8},{5,9},{6,10},{7,11},{8,4},{9,5},... | collective-permute-start | bytes 393224 | tf_op jit(solution)/shard_map/ppermute | solution.py:648
  413.0 51.8 %collective-permute-start.40 = (f32[1,2,2,64,128]{4,3,2,1,0:T(8,128)S(1)}, f32[1,2,2,64,128]{4,3,2,1,0:T(8,128)S(1)}, u32[]{:S(2)}, u32[]{:S(2)}) collective-permute-start(f32[1,2,2,64,128]{4,3,2,1,0:T(8,128)S(1)} %bitcast.132), channel_id=1, source_target_pairs={{0,11},{1,10},{2,9},{3,8},{4,15},{5,14},{6,13},{7,12},{8,3},{9,2},... | collective-permute-start | bytes 393224 | tf_op jit(solution)/shard_map/ppermute | solution.py:648
  448.0 21.7 %collective-permute-start.39 = (f32[1,2,2,64,128]{4,3,2,1,0:T(8,128)S(1)}, f32[1,2,2,64,128]{4,3,2,1,0:T(8,128)S(1)}, u32[]{:S(2)}, u32[]{:S(2)}) collective-permute-start(f32[1,2,2,64,128]{4,3,2,1,0:T(8,128)S(1)} %bitcast.128), channel_id=1, source_target_pairs={{0,10},{1,11},{2,8},{3,9},{4,14},{5,15},{6,12},{7,13},{8,2},{9,3},... | collective-permute-start | bytes 393224 | tf_op jit(solution)/shard_map/ppermute | solution.py:648
  451.7 21.5 %collective-permute-start.38 = (f32[1,2,2,64,128]{4,3,2,1,0:T(8,128)S(1)}, f32[1,2,2,64,128]{4,3,2,1,0:T(8,128)S(1)}, u32[]{:S(2)}, u32[]{:S(2)}) collective-permute-start(f32[1,2,2,64,128]{4,3,2,1,0:T(8,128)S(1)} %bitcast.124), channel_id=1, source_target_pairs={{0,9},{1,8},{2,11},{3,10},{4,13},{5,12},{6,15},{7,14},{8,1},{9,0},... | collective-permute-start | bytes 393224 | tf_op jit(solution)/shard_map/ppermute | solution.py:648
  459.2 15.3 %collective-permute-start.37 = (f32[1,2,2,64,128]{4,3,2,1,0:T(8,128)S(1)}, f32[1,2,2,64,128]{4,3,2,1,0:T(8,128)S(1)}, u32[]{:S(2)}, u32[]{:S(2)}) collective-permute-start(f32[1,2,2,64,128]{4,3,2,1,0:T(8,128)S(1)} %bitcast.120), channel_id=1, source_target_pairs={{0,8},{1,9},{2,10},{3,11},{4,12},{5,13},{6,14},{7,15},{8,0},{9,1},... | collective-permute-start | bytes 393224 | tf_op jit(solution)/shard_map/ppermute | solution.py:648
  461.1 14.3 %collective-permute-start.36 = (f32[1,2,2,64,128]{4,3,2,1,0:T(8,128)S(1)}, f32[1,2,2,64,128]{4,3,2,1,0:T(8,128)S(1)}, u32[]{:S(2)}, u32[]{:S(2)}) collective-permute-start(f32[1,2,2,64,128]{4,3,2,1,0:T(8,128)S(1)} %bitcast.116), channel_id=1, source_target_pairs={{0,7},{1,6},{2,5},{3,4},{4,3},{5,2},{6,1},{7,0},{8,15},{9,14},{10,... | collective-permute-start | bytes 393224 | tf_op jit(solution)/shard_map/ppermute | solution.py:648
  464.8 12.8 %collective-permute-start.35 = (f32[1,2,2,64,128]{4,3,2,1,0:T(8,128)S(1)}, f32[1,2,2,64,128]{4,3,2,1,0:T(8,128)S(1)}, u32[]{:S(2)}, u32[]{:S(2)}) collective-permute-start(f32[1,2,2,64,128]{4,3,2,1,0:T(8,128)S(1)} %bitcast.112), channel_id=1, source_target_pairs={{0,6},{1,7},{2,4},{3,5},{4,2},{5,3},{6,0},{7,1},{8,14},{9,15},{10,... | collective-permute-start | bytes 393224 | tf_op jit(solution)/shard_map/ppermute | solution.py:648
  501.6 12.2 %collective-permute-start.58 = (f32[1,2,2,64,128]{4,3,2,1,0:T(8,128)S(1)}, f32[1,2,2,64,128]{4,3,2,1,0:T(8,128)S(1)}, u32[]{:S(2)}, u32[]{:S(2)}) collective-permute-start(f32[1,2,2,64,128]{4,3,2,1,0:T(8,128)S(1)} %bitcast.149), channel_id=1, source_target_pairs={{0,14},{1,15},{2,12},{3,13},{4,10},{5,11},{6,8},{7,9},{8,6},{9,7},... | collective-permute-start | bytes 393224 | tf_op jit(solution)/shard_map/ppermute | solution.py:648
  502.7 25.5 %collective-permute-start.59 = (f32[1,2,2,64,128]{4,3,2,1,0:T(8,128)S(1)}, f32[1,2,2,64,128]{4,3,2,1,0:T(8,128)S(1)}, u32[]{:S(2)}, u32[]{:S(2)}) collective-permute-start(f32[1,2,2,64,128]{4,3,2,1,0:T(8,128)S(1)} %bitcast.145), channel_id=1, source_target_pairs={{0,15},{1,14},{2,13},{3,12},{4,11},{5,10},{6,9},{7,8},{8,7},{9,6},... | collective-permute-start | bytes 393224 | tf_op jit(solution)/shard_map/ppermute | solution.py:648
  504.5 30.9 %collective-permute-start.57 = (f32[1,2,2,64,128]{4,3,2,1,0:T(8,128)S(1)}, f32[1,2,2,64,128]{4,3,2,1,0:T(8,128)S(1)}, u32[]{:S(2)}, u32[]{:S(2)}) collective-permute-start(f32[1,2,2,64,128]{4,3,2,1,0:T(8,128)S(1)} %bitcast.141), channel_id=1, source_target_pairs={{0,13},{1,12},{2,15},{3,14},{4,9},{5,8},{6,11},{7,10},{8,5},{9,4},... | collective-permute-start | bytes 393224 | tf_op jit(solution)/shard_map/ppermute | solution.py:648
  504.6 32.1 %collective-permute-start.56 = (f32[1,2,2,64,128]{4,3,2,1,0:T(8,128)S(1)}, f32[1,2,2,64,128]{4,3,2,1,0:T(8,128)S(1)}, u32[]{:S(2)}, u32[]{:S(2)}) collective-permute-start(f32[1,2,2,64,128]{4,3,2,1,0:T(8,128)S(1)} %bitcast.137), channel_id=1, source_target_pairs={{0,12},{1,13},{2,14},{3,15},{4,8},{5,9},{6,10},{7,11},{8,4},{9,5},... | collective-permute-start | bytes 393224 | tf_op jit(solution)/shard_map/ppermute | solution.py:648
  505.7 33.0 %collective-permute-start.55 = (f32[1,2,2,64,128]{4,3,2,1,0:T(8,128)S(1)}, f32[1,2,2,64,128]{4,3,2,1,0:T(8,128)S(1)}, u32[]{:S(2)}, u32[]{:S(2)}) collective-permute-start(f32[1,2,2,64,128]{4,3,2,1,0:T(8,128)S(1)} %bitcast.133), channel_id=1, source_target_pairs={{0,11},{1,10},{2,9},{3,8},{4,15},{5,14},{6,13},{7,12},{8,3},{9,2},... | collective-permute-start | bytes 393224 | tf_op jit(solution)/shard_map/ppermute | solution.py:648
  513.8 30.7 %collective-permute-start.54 = (f32[1,2,2,64,128]{4,3,2,1,0:T(8,128)S(1)}, f32[1,2,2,64,128]{4,3,2,1,0:T(8,128)S(1)}, u32[]{:S(2)}, u32[]{:S(2)}) collective-permute-start(f32[1,2,2,64,128]{4,3,2,1,0:T(8,128)S(1)} %bitcast.129), channel_id=1, source_target_pairs={{0,10},{1,11},{2,8},{3,9},{4,14},{5,15},{6,12},{7,13},{8,2},{9,3},... | collective-permute-start | bytes 393224 | tf_op jit(solution)/shard_map/ppermute | solution.py:648
  528.2 18.7 %collective-permute-start.53 = (f32[1,2,2,64,128]{4,3,2,1,0:T(8,128)S(1)}, f32[1,2,2,64,128]{4,3,2,1,0:T(8,128)S(1)}, u32[]{:S(2)}, u32[]{:S(2)}) collective-permute-start(f32[1,2,2,64,128]{4,3,2,1,0:T(8,128)S(1)} %bitcast.125), channel_id=1, source_target_pairs={{0,9},{1,8},{2,11},{3,10},{4,13},{5,12},{6,15},{7,14},{8,1},{9,0},... | collective-permute-start | bytes 393224 | tf_op jit(solution)/shard_map/ppermute | solution.py:648
  535.4 13.8 %collective-permute-start.52 = (f32[1,2,2,64,128]{4,3,2,1,0:T(8,128)S(1)}, f32[1,2,2,64,128]{4,3,2,1,0:T(8,128)S(1)}, u32[]{:S(2)}, u32[]{:S(2)}) collective-permute-start(f32[1,2,2,64,128]{4,3,2,1,0:T(8,128)S(1)} %bitcast.121), channel_id=1, source_target_pairs={{0,8},{1,9},{2,10},{3,11},{4,12},{5,13},{6,14},{7,15},{8,0},{9,1},... | collective-permute-start | bytes 393224 | tf_op jit(solution)/shard_map/ppermute | solution.py:648
  536.7 12.5 %collective-permute-start.51 = (f32[1,2,2,64,128]{4,3,2,1,0:T(8,128)S(1)}, f32[1,2,2,64,128]{4,3,2,1,0:T(8,128)S(1)}, u32[]{:S(2)}, u32[]{:S(2)}) collective-permute-start(f32[1,2,2,64,128]{4,3,2,1,0:T(8,128)S(1)} %bitcast.117), channel_id=1, source_target_pairs={{0,7},{1,6},{2,5},{3,4},{4,3},{5,2},{6,1},{7,0},{8,15},{9,14},{10,... | collective-permute-start | bytes 393224 | tf_op jit(solution)/shard_map/ppermute | solution.py:648
  538.8 13.3 %collective-permute-start.50 = (f32[1,2,2,64,128]{4,3,2,1,0:T(8,128)S(1)}, f32[1,2,2,64,128]{4,3,2,1,0:T(8,128)S(1)}, u32[]{:S(2)}, u32[]{:S(2)}) collective-permute-start(f32[1,2,2,64,128]{4,3,2,1,0:T(8,128)S(1)} %bitcast.113), channel_id=1, source_target_pairs={{0,6},{1,7},{2,4},{3,5},{4,2},{5,3},{6,0},{7,1},{8,14},{9,15},{10,... | collective-permute-start | bytes 393224 | tf_op jit(solution)/shard_map/ppermute | solution.py:648
  544.5 15.9 %collective-permute-start.49 = (f32[1,2,2,64,128]{4,3,2,1,0:T(8,128)}, f32[1,2,2,64,128]{4,3,2,1,0:T(8,128)S(1)}, u32[]{:S(2)}, u32[]{:S(2)}) collective-permute-start(f32[1,2,2,64,128]{4,3,2,1,0:T(8,128)} %bitcast.63), channel_id=1, source_target_pairs={{0,5},{1,4},{2,7},{3,6},{4,1},{5,0},{6,3},{7,2},{8,13},{9,12},{10,... | collective-permute-start | bytes 393224 | tf_op jit(solution)/shard_map/ppermute | solution.py:648
  547.0 13.4 %collective-permute-start.48 = (f32[1,2,2,64,128]{4,3,2,1,0:T(8,128)}, f32[1,2,2,64,128]{4,3,2,1,0:T(8,128)S(1)}, u32[]{:S(2)}, u32[]{:S(2)}) collective-permute-start(f32[1,2,2,64,128]{4,3,2,1,0:T(8,128)} %bitcast.62), channel_id=1, source_target_pairs={{0,4},{1,5},{2,6},{3,7},{4,0},{5,1},{6,2},{7,3},{8,12},{9,13},{10,... | collective-permute-start | bytes 393224 | tf_op jit(solution)/shard_map/ppermute | solution.py:648
  549.2 11.1 %collective-permute-start.47 = (f32[1,2,2,64,128]{4,3,2,1,0:T(8,128)}, f32[1,2,2,64,128]{4,3,2,1,0:T(8,128)S(1)}, u32[]{:S(2)}, u32[]{:S(2)}) collective-permute-start(f32[1,2,2,64,128]{4,3,2,1,0:T(8,128)} %bitcast.61), channel_id=1, source_target_pairs={{0,3},{1,2},{2,1},{3,0},{4,7},{5,6},{6,5},{7,4},{8,11},{9,10},{10,... | collective-permute-start | bytes 393224 | tf_op jit(solution)/shard_map/ppermute | solution.py:648
  549.2 11.1 %collective-permute-start.46 = (f32[1,2,2,64,128]{4,3,2,1,0:T(8,128)}, f32[1,2,2,64,128]{4,3,2,1,0:T(8,128)S(1)}, u32[]{:S(2)}, u32[]{:S(2)}) collective-permute-start(f32[1,2,2,64,128]{4,3,2,1,0:T(8,128)} %bitcast.60), channel_id=1, source_target_pairs={{0,2},{1,3},{2,0},{3,1},{4,6},{5,7},{6,4},{7,5},{8,10},{9,11},{10,... | collective-permute-start | bytes 393224 | tf_op jit(solution)/shard_map/ppermute | solution.py:648
  (84 other events, 683.3 us)

commit v2 on v1

--- a/solution.py
+++ b/solution.py
@@ -232,16 +232,20 @@
     chosen = chosen_nodes(count, size)
     made = ((high_buf, made_high), (low_buf, made_low))
 
-    def step(t, carry):
+    def piece(t):
         part = pl.ds(pl.multiple_of(t * rows, rows), rows)
         build_rows(count, part, inputs, chosen, high_buf.at[part], low_buf.at[part])
         for n, (buf, to) in enumerate(made):
             pltpu.make_async_copy(buf.at[part], to.at[part], map_sems.at[n, t]).start()
         value = interpolate(high_buf.at[part], low_buf.at[part], m_high, m_low, dot_nt)
         finish_rows(flip_ref[0], t, value, held_ref, out_ref, sems)
+
+    def step(t, carry):
+        piece(2 * t)
+        piece(2 * t + 1)
         return carry
 
-    lax.fori_loop(0, PIECES, step, 0)
+    lax.fori_loop(0, PIECES // 2, step, 0)
     finish_copies(held_ref, out_ref, sems)
     for t in range(PIECES):
         part = pl.ds(t * rows, rows)
@@ -800,6 +804,7 @@
 
     def body(source, green, *rest):
         whole_rows = source.shape[0] % 4 == 0 and green.shape[0] % 4 == 0
+        whole_rows = whole_rows and devices >= PIECES and devices & (devices - 1) == 0
         chosen = shards if whole_rows and source.shape[1] == LANES else shards_by_row
         return chosen(devices, source, green, *rest)
 

time: 582 us -> 582 us (level)
  no operation moved by 1% of the time
where the time goes in v2:
time: 582 us; the launch traced here: 577 us
  waiting for transfers between devices  211 us (36%)
  Pallas kernels  146 us (25%)
  starting transfers between devices  118 us (20%)
  blocking collectives  55.5 us (10%)
  local copies, waits for them, and re-layouts  45.4 us (8%)
    ppermute x60, waiting for transfers between devices, exchange(): arrived.append(lax.ppermute(sent[s:s + 1], 'mom', route))  178 us
    pallas_call x13, Pallas kernels, call(): pl.pallas_call(kernel, grid_spec=pltpu.PrefetchScalarGridSpec(num_scalar_...  146 us
    ppermute x60, starting transfers between devices, exchange(): arrived.append(lax.ppermute(sent[s:s + 1], 'mom', route))  100 us
    all_to_all x1, blocking collectives, exchange(): return lax.all_to_all(sent, 'mom', split_axis=0, concat_axis=0, tiled=True)  55.5 us
    unnamed x140, local copies, waits for them, and re-layouts  35.3 us
    all_to_all x3, waiting for transfers between devices, exchange(): return lax.all_to_all(sent, 'mom', split_axis=0, concat_axis=0, tiled=True)  32.9 us
    all_to_all x3, starting transfers between devices, exchange(): return lax.all_to_all(sent, 'mom', split_axis=0, concat_axis=0, tiled=True)  17.5 us
  transfers between devices with their start and end apart: 63, of which 28 were waited for; matrix products, arithmetic and copies ran while one was open for 2% of the time, Pallas kernels for 11%

profile of v2, /device:TPU:9, one launch (start us, length us, event | category | flops | bytes accessed | tf_op | source)
XLA Modules:
  0.0 577.3 jit_solution(16054748593338469046)
XLA Ops:
  1.8 17.9 %shard_map.131 = (f32[16,2,2,2,32,128]{5,4,3,2,1,0:T(8,128)}, bf16[1024,2048]{1,0:T(8,128)(2,1)}, bf16[1024,2048]{1,0:T(8,128)(2,1)}) custom-call(s32[2]{0:T(128)} %pad_add_fusion.1.flip_ref, f32[8,128,1024]{2,1,0:T(8,128)} %source_ref.7, f32[2,4,128,128]{3,2,1,0:T(8,128)} %refs_17_.3, s32[2,1024]{1,0:T(2,128)} %refs_0_.1, s32[2,1024]{1,0:T(2,128)} %refs_1_.2, ...), custom_call_target="tpu_custom_call" | custom-call | flops 7247757312 | bytes 12582912 | tf_op jit(solution)/shard_map/pallas_call | solution.py:35
  19.8 13.5 %shard_map.132 = f32[16,2,2,2,32,128]{5,4,3,2,1,0:T(8,128)} custom-call(s32[2]{0:T(128)} %pad_add_fusion.flip_ref, f32[8,128,1024]{2,1,0:T(8,128)} %source_ref.7, f32[2,4,128,128]{3,2,1,0:T(8,128)} %refs_17_.3, bf16[1024,2048]{1,0:T(8,128)(2,1)} %get-tuple-element.7.high_ref.refs_18_, bf16[1024,2048]{1,0:T(8,128)(2,1)} %get-tuple-element.8.low_ref.refs_19_), custom_call_target="tpu_custom_call" | custom-call | flops 7247757312 | bytes 12582912 | tf_op jit(solution)/shard_map/pallas_call | solution.py:35
  33.3 6.7 %all-to-all-start = ((f32[16,2,2,64,128]{4,3,2,1,0:T(8,128)}), f32[16,2,2,64,128]{4,3,2,1,0:T(8,128)S(1)}, u32[]{:S(2)}, u32[]{:S(2)}) async-start(f32[16,2,2,64,128]{4,3,2,1,0:T(8,128)} %bitcast.89), calls=%async_computation | async-start | bytes 4194304 | tf_op jit(solution)/shard_map/all_to_all | solution.py:648
  44.9 8.3 %shard_map.133 = (bf16[1024,2048]{1,0:T(8,128)(2,1)}, bf16[1024,2048]{1,0:T(8,128)(2,1)}) custom-call(s32[2,1024]{1,0:T(2,128)} %reshape.123.refs_0_, s32[2,1024]{1,0:T(2,128)} %reshape.125.refs_1_, f32[2,4,1024]{2,1,0:T(4,128)} %reshape.127.refs_2_, f32[2,4,1024]{2,1,0:T(4,128)} %reshape.129.refs_3_), custom_call_target="tpu_custom_call" | custom-call | flops 20971520 | bytes 8388608 | tf_op jit(solution)/shard_map/pallas_call | solution.py:35
  53.2 32.9 %all-to-all-done.refs_0_ = f32[16,2,2,64,128]{4,3,2,1,0:T(8,128)S(1)} async-done(((f32[16,2,2,64,128]{4,3,2,1,0:T(8,128)}), f32[16,2,2,64,128]{4,3,2,1,0:T(8,128)S(1)}, u32[]{:S(2)}, u32[]{:S(2)}) %all-to-all-start) | async-done | bytes 2097184 | tf_op jit(solution)/shard_map/all_to_all | solution.py:648
  87.4 14.4 %shard_map.135 = f32[16,2,2,2,32,128]{5,4,3,2,1,0:T(8,128)} custom-call(s32[2]{0:T(128)} %pad_add_fusion.flip_ref, f32[16,2,2,64,128]{4,3,2,1,0:T(8,128)} %copy-done.38, f32[2,4,128,128]{3,2,1,0:T(8,128)} %refs_32_.1, f32[1024,4]{1,0:T(8,128)} %copy.29.refs_2_.refs_3_, bf16[1024,2048]{1,0:T(8,128)(2,1)} %get-tuple-element.10.refs_18_.refs_3_.refs_4_.refs_34_, ...), custom_call_target="tpu_custom_call" | custom-call | flops 7247757312 | bytes 10485760 | tf_op jit(solution)/shard_map/pallas_call | solution.py:35
  101.8 6.1 %all-to-all-start.1 = ((f32[16,2,2,64,128]{4,3,2,1,0:T(8,128)}), f32[16,2,2,64,128]{4,3,2,1,0:T(8,128)S(1)}, u32[]{:S(2)}, u32[]{:S(2)}) async-start(f32[16,2,2,64,128]{4,3,2,1,0:T(8,128)} %bitcast.88), calls=%async_computation.1 | async-start | bytes 4194304 | tf_op jit(solution)/shard_map/all_to_all | solution.py:648
  113.8 7.4 %collective-permute-start.10 = (f32[1,2,2,64,128]{4,3,2,1,0:T(8,128)S(1)}, f32[1,2,2,64,128]{4,3,2,1,0:T(8,128)S(1)}, u32[]{:S(2)}, u32[]{:S(2)}) collective-permute-start(f32[1,2,2,64,128]{4,3,2,1,0:T(8,128)S(1)} %bitcast.130), channel_id=1, source_target_pairs={{0,11},{1,10},{2,9},{3,8},{4,15},{5,14},{6,13},{7,12},{8,3},{9,2},... | collective-permute-start | bytes 393224 | tf_op jit(solution)/shard_map/ppermute | solution.py:652
  121.2 51.5 %collective-permute-done.13.refs_14_ = f32[1,2,2,64,128]{4,3,2,1,0:T(8,128)S(1)} collective-permute-done((f32[1,2,2,64,128]{4,3,2,1,0:T(8,128)S(1)}, f32[1,2,2,64,128]{4,3,2,1,0:T(8,128)S(1)}, u32[]{:S(2)}, u32[]{:S(2)}) %collective-permute-start.13) | collective-permute-done | bytes 131104 | tf_op jit(solution)/shard_map/ppermute | solution.py:652
  172.8 3.7 collective-permute-done.14.refs_15_
  176.8 7.1 %collective-permute-done.12.refs_13_ = f32[1,2,2,64,128]{4,3,2,1,0:T(8,128)S(1)} collective-permute-done((f32[1,2,2,64,128]{4,3,2,1,0:T(8,128)S(1)}, f32[1,2,2,64,128]{4,3,2,1,0:T(8,128)S(1)}, u32[]{:S(2)}, u32[]{:S(2)}) %collective-permute-start.12) | collective-permute-done | bytes 131104 | tf_op jit(solution)/shard_map/ppermute | solution.py:652
  186.2 3.4 collective-permute-done.10.refs_11_
  189.6 5.0 collective-permute-start.5
  194.5 3.4 collective-permute-start.4
  205.2 2.8 collective-permute-done.3.refs_4_
  208.1 14.6 %shard_map.134 = f32[16,2,2,2,32,128]{5,4,3,2,1,0:T(8,128)} custom-call(s32[2]{0:T(128)} %pad_add_fusion.1.flip_ref, f32[16,2,2,64,128]{4,3,2,1,0:T(8,128)} %bitcast.90, f32[1,2,2,64,128]{4,3,2,1,0:T(8,128)} %collective-permute-done.refs_1_, f32[1,2,2,64,128]{4,3,2,1,0:T(8,128)} %collective-permute-done.1.refs_2_, ...), custom_call_target="tpu_custom_call" | custom-call | flops 7247757312 | bytes 10485760 | tf_op jit(solution)/shard_map/pallas_call | solution.py:35
  228.6 8.3 %collective-permute-start.25 = (f32[1,2,2,64,128]{4,3,2,1,0:T(8,128)S(1)}, f32[1,2,2,64,128]{4,3,2,1,0:T(8,128)S(1)}, u32[]{:S(2)}, u32[]{:S(2)}) collective-permute-start(f32[1,2,2,64,128]{4,3,2,1,0:T(8,128)S(1)} %bitcast.131), channel_id=1, source_target_pairs={{0,11},{1,10},{2,9},{3,8},{4,15},{5,14},{6,13},{7,12},{8,3},{9,2},... | collective-permute-start | bytes 393224 | tf_op jit(solution)/shard_map/ppermute | solution.py:652
  236.9 14.2 %collective-permute-done.29.refs_15_ = f32[1,2,2,64,128]{4,3,2,1,0:T(8,128)S(1)} collective-permute-done((f32[1,2,2,64,128]{4,3,2,1,0:T(8,128)S(1)}, f32[1,2,2,64,128]{4,3,2,1,0:T(8,128)S(1)}, u32[]{:S(2)}, u32[]{:S(2)}) %collective-permute-start.29) | collective-permute-done | bytes 131104 | tf_op jit(solution)/shard_map/ppermute | solution.py:652
  251.2 7.2 %collective-permute-done.27.refs_13_ = f32[1,2,2,64,128]{4,3,2,1,0:T(8,128)S(1)} collective-permute-done((f32[1,2,2,64,128]{4,3,2,1,0:T(8,128)S(1)}, f32[1,2,2,64,128]{4,3,2,1,0:T(8,128)S(1)}, u32[]{:S(2)}, u32[]{:S(2)}) %collective-permute-start.27) | collective-permute-done | bytes 131104 | tf_op jit(solution)/shard_map/ppermute | solution.py:652
  261.8 5.6 collective-permute-start.20
  267.4 2.4 collective-permute-start.19
  275.7 3.0 collective-permute-start.15
  293.0 14.3 %shard_map.136 = f32[16,2,2,2,32,128]{5,4,3,2,1,0:T(8,128)S(1)} custom-call(s32[2]{0:T(128)S(1)} %copy-done.8, f32[16,2,2,64,128]{4,3,2,1,0:T(8,128)S(1)} %bitcast.85, f32[1,2,2,64,128]{4,3,2,1,0:T(8,128)S(1)} %copy-done.36, f32[1,2,2,64,128]{4,3,2,1,0:T(8,128)S(1)} %copy-done.33, f32[1,2,2,64,128]{4,3,2,1,0:T(8,128)S(1)} %copy-done.30, ...), custom_call_target="tpu_custom_call" | custom-call | flops 9663676416 | bytes 12582912 | tf_op jit(solution)/shard_map/pallas_call | solution.py:35
  307.3 55.5 %all_to_all.20.refs_1_ = f32[16,2,2,64,128]{4,3,2,1,0:T(8,128)} all-to-all(f32[16,2,2,64,128]{4,3,2,1,0:T(8,128)S(1)} %bitcast.83), channel_id=1, replica_groups=mesh['energy'=2,'mom'=16] {'mom'}, dimensions={0} | all-to-all | bytes 4194304 | tf_op jit(solution)/shard_map/all_to_all | solution.py:648
  362.8 15.0 %shard_map.137.sent_ref = f32[16,2,2,2,32,128]{5,4,3,2,1,0:T(8,128)} custom-call(s32[2]{0:T(128)} %pad_add_fusion.flip_ref, f32[16,2,2,64,128]{4,3,2,1,0:T(8,128)} %copy-done.38, f32[16,2,2,64,128]{4,3,2,1,0:T(8,128)} %all_to_all.20.refs_1_, f32[2,4,128,128]{3,2,1,0:T(8,128)} %refs_32_.1, f32[1024,4]{1,0:T(8,128)} %copy.29.refs_2_.refs_3_, ...), custom_call_target="tpu_custom_call" | custom-call | flops 7247757312 | bytes 12582912 | tf_op jit(solution)/shard_map/pallas_call | solution.py:35
  377.8 4.6 all-to-all-start.3
  392.2 14.3 %shard_map.138 = f32[16,2,2,2,32,128]{5,4,3,2,1,0:T(8,128)S(1)} custom-call(s32[2]{0:T(128)S(1)} %copy-done.6, f32[16,2,2,64,128]{4,3,2,1,0:T(8,128)S(1)} %bitcast.86, f32[1,2,2,64,128]{4,3,2,1,0:T(8,128)S(1)} %copy-done.37, f32[1,2,2,64,128]{4,3,2,1,0:T(8,128)S(1)} %copy-done.34, f32[1,2,2,64,128]{4,3,2,1,0:T(8,128)S(1)} %copy-done.31, ...), custom_call_target="tpu_custom_call" | custom-call | flops 9663676416 | bytes 12582912 | tf_op jit(solution)/shard_map/pallas_call | solution.py:35
  412.1 7.4 %collective-permute-start.40 = (f32[1,2,2,64,128]{4,3,2,1,0:T(8,128)S(1)}, f32[1,2,2,64,128]{4,3,2,1,0:T(8,128)S(1)}, u32[]{:S(2)}, u32[]{:S(2)}) collective-permute-start(f32[1,2,2,64,128]{4,3,2,1,0:T(8,128)S(1)} %bitcast.132), channel_id=1, source_target_pairs={{0,11},{1,10},{2,9},{3,8},{4,15},{5,14},{6,13},{7,12},{8,3},{9,2},... | collective-permute-start | bytes 393224 | tf_op jit(solution)/shard_map/ppermute | solution.py:652
  419.6 27.7 %collective-permute-done.43.refs_30_ = f32[1,2,2,64,128]{4,3,2,1,0:T(8,128)S(1)} collective-permute-done((f32[1,2,2,64,128]{4,3,2,1,0:T(8,128)S(1)}, f32[1,2,2,64,128]{4,3,2,1,0:T(8,128)S(1)}, u32[]{:S(2)}, u32[]{:S(2)}) %collective-permute-start.43) | collective-permute-done | bytes 131104 | tf_op jit(solution)/shard_map/ppermute | solution.py:652
  447.3 3.7 collective-permute-done.44.refs_31_
  451.3 7.1 %collective-permute-done.42.refs_29_ = f32[1,2,2,64,128]{4,3,2,1,0:T(8,128)S(1)} collective-permute-done((f32[1,2,2,64,128]{4,3,2,1,0:T(8,128)S(1)}, f32[1,2,2,64,128]{4,3,2,1,0:T(8,128)S(1)}, u32[]{:S(2)}, u32[]{:S(2)}) %collective-permute-start.42) | collective-permute-done | bytes 131104 | tf_op jit(solution)/shard_map/ppermute | solution.py:652
  460.7 3.4 collective-permute-done.40.refs_27_
  464.1 5.0 collective-permute-start.35
  469.1 3.4 collective-permute-start.34
  477.3 2.4 collective-permute-done.34.refs_21_
  479.7 2.8 collective-permute-done.33.refs_20_
  483.3 15.0 %shard_map.139.sent_ref = f32[16,2,2,2,32,128]{5,4,3,2,1,0:T(8,128)} custom-call(s32[2]{0:T(128)} %pad_add_fusion.1.flip_ref, f32[16,2,2,64,128]{4,3,2,1,0:T(8,128)} %bitcast.91, f32[1,2,2,64,128]{4,3,2,1,0:T(8,128)} %collective-permute-done.refs_1_, f32[1,2,2,64,128]{4,3,2,1,0:T(8,128)} %collective-permute-done.1.refs_2_, ...), custom_call_target="tpu_custom_call" | custom-call | flops 7247757312 | bytes 12582912 | tf_op jit(solution)/shard_map/pallas_call | solution.py:35
  498.4 2.5 fusion
  505.0 8.1 %collective-permute-start.55 = (f32[1,2,2,64,128]{4,3,2,1,0:T(8,128)S(1)}, f32[1,2,2,64,128]{4,3,2,1,0:T(8,128)S(1)}, u32[]{:S(2)}, u32[]{:S(2)}) collective-permute-start(f32[1,2,2,64,128]{4,3,2,1,0:T(8,128)S(1)} %bitcast.133), channel_id=1, source_target_pairs={{0,11},{1,10},{2,9},{3,8},{4,15},{5,14},{6,13},{7,12},{8,3},{9,2},... | collective-permute-start | bytes 393224 | tf_op jit(solution)/shard_map/ppermute | solution.py:652
  513.1 14.4 %collective-permute-done.59.refs_15_ = f32[1,2,2,64,128]{4,3,2,1,0:T(8,128)S(1)} collective-permute-done((f32[1,2,2,64,128]{4,3,2,1,0:T(8,128)S(1)}, f32[1,2,2,64,128]{4,3,2,1,0:T(8,128)S(1)}, u32[]{:S(2)}, u32[]{:S(2)}) %collective-permute-start.59) | collective-permute-done | bytes 131104 | tf_op jit(solution)/shard_map/ppermute | solution.py:652
  527.5 7.2 %collective-permute-done.57.refs_13_ = f32[1,2,2,64,128]{4,3,2,1,0:T(8,128)S(1)} collective-permute-done((f32[1,2,2,64,128]{4,3,2,1,0:T(8,128)S(1)}, f32[1,2,2,64,128]{4,3,2,1,0:T(8,128)S(1)}, u32[]{:S(2)}, u32[]{:S(2)}) %collective-permute-start.57) | collective-permute-done | bytes 131104 | tf_op jit(solution)/shard_map/ppermute | solution.py:652
  538.1 5.8 collective-permute-start.50
  543.8 2.4 collective-permute-start.49
  551.4 3.0 collective-permute-start.45
  554.4 5.3 shard_map.142.refs_0_
  561.9 3.0 shard_map.140.refs_1_
  564.9 5.4 shard_map.143
  572.5 4.8 shard_map.141
  (254 shorter events, 93.2 us)
Async XLA Ops:
  33.3 52.8 %all-to-all-start = ((f32[16,2,2,64,128]{4,3,2,1,0:T(8,128)}), f32[16,2,2,64,128]{4,3,2,1,0:T(8,128)S(1)}, u32[]{:S(2)}, u32[]{:S(2)}) async-start(f32[16,2,2,64,128]{4,3,2,1,0:T(8,128)} %bitcast.89), calls=%async_computation | async-start | bytes 4194304 | tf_op jit(solution)/shard_map/all_to_all | solution.py:648
  101.8 181.4 %all-to-all-start.1 = ((f32[16,2,2,64,128]{4,3,2,1,0:T(8,128)}), f32[16,2,2,64,128]{4,3,2,1,0:T(8,128)S(1)}, u32[]{:S(2)}, u32[]{:S(2)}) async-start(f32[16,2,2,64,128]{4,3,2,1,0:T(8,128)} %bitcast.88), calls=%async_computation.1 | async-start | bytes 4194304 | tf_op jit(solution)/shard_map/all_to_all | solution.py:648
  109.6 63.1 %collective-permute-start.13 = (f32[1,2,2,64,128]{4,3,2,1,0:T(8,128)S(1)}, f32[1,2,2,64,128]{4,3,2,1,0:T(8,128)S(1)}, u32[]{:S(2)}, u32[]{:S(2)}) collective-permute-start(f32[1,2,2,64,128]{4,3,2,1,0:T(8,128)S(1)} %bitcast.146), channel_id=1, source_target_pairs={{0,14},{1,15},{2,12},{3,13},{4,10},{5,11},{6,8},{7,9},{8,6},{9,7},... | collective-permute-start | bytes 393224 | tf_op jit(solution)/shard_map/ppermute | solution.py:652
  111.8 64.7 %collective-permute-start.14 = (f32[1,2,2,64,128]{4,3,2,1,0:T(8,128)S(1)}, f32[1,2,2,64,128]{4,3,2,1,0:T(8,128)S(1)}, u32[]{:S(2)}, u32[]{:S(2)}) collective-permute-start(f32[1,2,2,64,128]{4,3,2,1,0:T(8,128)S(1)} %bitcast.142), channel_id=1, source_target_pairs={{0,15},{1,14},{2,13},{3,12},{4,11},{5,10},{6,9},{7,8},{8,7},{9,6},... | collective-permute-start | bytes 393224 | tf_op jit(solution)/shard_map/ppermute | solution.py:652
  112.6 71.3 %collective-permute-start.12 = (f32[1,2,2,64,128]{4,3,2,1,0:T(8,128)S(1)}, f32[1,2,2,64,128]{4,3,2,1,0:T(8,128)S(1)}, u32[]{:S(2)}, u32[]{:S(2)}) collective-permute-start(f32[1,2,2,64,128]{4,3,2,1,0:T(8,128)S(1)} %bitcast.138), channel_id=1, source_target_pairs={{0,13},{1,12},{2,15},{3,14},{4,9},{5,8},{6,11},{7,10},{8,5},{9,4},... | collective-permute-start | bytes 393224 | tf_op jit(solution)/shard_map/ppermute | solution.py:652
  113.5 72.3 %collective-permute-start.11 = (f32[1,2,2,64,128]{4,3,2,1,0:T(8,128)S(1)}, f32[1,2,2,64,128]{4,3,2,1,0:T(8,128)S(1)}, u32[]{:S(2)}, u32[]{:S(2)}) collective-permute-start(f32[1,2,2,64,128]{4,3,2,1,0:T(8,128)S(1)} %bitcast.134), channel_id=1, source_target_pairs={{0,12},{1,13},{2,14},{3,15},{4,8},{5,9},{6,10},{7,11},{8,4},{9,5},... | collective-permute-start | bytes 393224 | tf_op jit(solution)/shard_map/ppermute | solution.py:652
  113.8 75.8 %collective-permute-start.10 = (f32[1,2,2,64,128]{4,3,2,1,0:T(8,128)S(1)}, f32[1,2,2,64,128]{4,3,2,1,0:T(8,128)S(1)}, u32[]{:S(2)}, u32[]{:S(2)}) collective-permute-start(f32[1,2,2,64,128]{4,3,2,1,0:T(8,128)S(1)} %bitcast.130), channel_id=1, source_target_pairs={{0,11},{1,10},{2,9},{3,8},{4,15},{5,14},{6,13},{7,12},{8,3},{9,2},... | collective-permute-start | bytes 393224 | tf_op jit(solution)/shard_map/ppermute | solution.py:652
  172.8 21.7 %collective-permute-start.9 = (f32[1,2,2,64,128]{4,3,2,1,0:T(8,128)S(1)}, f32[1,2,2,64,128]{4,3,2,1,0:T(8,128)S(1)}, u32[]{:S(2)}, u32[]{:S(2)}) collective-permute-start(f32[1,2,2,64,128]{4,3,2,1,0:T(8,128)S(1)} %bitcast.126), channel_id=1, source_target_pairs={{0,10},{1,11},{2,8},{3,9},{4,14},{5,15},{6,12},{7,13},{8,2},{9,3},... | collective-permute-start | bytes 393224 | tf_op jit(solution)/shard_map/ppermute | solution.py:652
  176.4 21.5 %collective-permute-start.8 = (f32[1,2,2,64,128]{4,3,2,1,0:T(8,128)S(1)}, f32[1,2,2,64,128]{4,3,2,1,0:T(8,128)S(1)}, u32[]{:S(2)}, u32[]{:S(2)}) collective-permute-start(f32[1,2,2,64,128]{4,3,2,1,0:T(8,128)S(1)} %bitcast.122), channel_id=1, source_target_pairs={{0,9},{1,8},{2,11},{3,10},{4,13},{5,12},{6,15},{7,14},{8,1},{9,0},... | collective-permute-start | bytes 393224 | tf_op jit(solution)/shard_map/ppermute | solution.py:652
  183.9 15.3 %collective-permute-start.7 = (f32[1,2,2,64,128]{4,3,2,1,0:T(8,128)S(1)}, f32[1,2,2,64,128]{4,3,2,1,0:T(8,128)S(1)}, u32[]{:S(2)}, u32[]{:S(2)}) collective-permute-start(f32[1,2,2,64,128]{4,3,2,1,0:T(8,128)S(1)} %bitcast.118), channel_id=1, source_target_pairs={{0,8},{1,9},{2,10},{3,11},{4,12},{5,13},{6,14},{7,15},{8,0},{9,1},... | collective-permute-start | bytes 393224 | tf_op jit(solution)/shard_map/ppermute | solution.py:652
  185.9 14.3 %collective-permute-start.6 = (f32[1,2,2,64,128]{4,3,2,1,0:T(8,128)S(1)}, f32[1,2,2,64,128]{4,3,2,1,0:T(8,128)S(1)}, u32[]{:S(2)}, u32[]{:S(2)}) collective-permute-start(f32[1,2,2,64,128]{4,3,2,1,0:T(8,128)S(1)} %bitcast.114), channel_id=1, source_target_pairs={{0,7},{1,6},{2,5},{3,4},{4,3},{5,2},{6,1},{7,0},{8,15},{9,14},{10,... | collective-permute-start | bytes 393224 | tf_op jit(solution)/shard_map/ppermute | solution.py:652
  189.6 12.8 %collective-permute-start.5 = (f32[1,2,2,64,128]{4,3,2,1,0:T(8,128)S(1)}, f32[1,2,2,64,128]{4,3,2,1,0:T(8,128)S(1)}, u32[]{:S(2)}, u32[]{:S(2)}) collective-permute-start(f32[1,2,2,64,128]{4,3,2,1,0:T(8,128)S(1)} %bitcast.110), channel_id=1, source_target_pairs={{0,6},{1,7},{2,4},{3,5},{4,2},{5,3},{6,0},{7,1},{8,14},{9,15},{10,... | collective-permute-start | bytes 393224 | tf_op jit(solution)/shard_map/ppermute | solution.py:652
  224.5 12.4 %collective-permute-start.28 = (f32[1,2,2,64,128]{4,3,2,1,0:T(8,128)S(1)}, f32[1,2,2,64,128]{4,3,2,1,0:T(8,128)S(1)}, u32[]{:S(2)}, u32[]{:S(2)}) collective-permute-start(f32[1,2,2,64,128]{4,3,2,1,0:T(8,128)S(1)} %bitcast.147), channel_id=1, source_target_pairs={{0,14},{1,15},{2,12},{3,13},{4,10},{5,11},{6,8},{7,9},{8,6},{9,7},... | collective-permute-start | bytes 393224 | tf_op jit(solution)/shard_map/ppermute | solution.py:652
  225.8 25.4 %collective-permute-start.29 = (f32[1,2,2,64,128]{4,3,2,1,0:T(8,128)S(1)}, f32[1,2,2,64,128]{4,3,2,1,0:T(8,128)S(1)}, u32[]{:S(2)}, u32[]{:S(2)}) collective-permute-start(f32[1,2,2,64,128]{4,3,2,1,0:T(8,128)S(1)} %bitcast.143), channel_id=1, source_target_pairs={{0,15},{1,14},{2,13},{3,12},{4,11},{5,10},{6,9},{7,8},{8,7},{9,6},... | collective-permute-start | bytes 393224 | tf_op jit(solution)/shard_map/ppermute | solution.py:652
  227.4 30.9 %collective-permute-start.27 = (f32[1,2,2,64,128]{4,3,2,1,0:T(8,128)S(1)}, f32[1,2,2,64,128]{4,3,2,1,0:T(8,128)S(1)}, u32[]{:S(2)}, u32[]{:S(2)}) collective-permute-start(f32[1,2,2,64,128]{4,3,2,1,0:T(8,128)S(1)} %bitcast.139), channel_id=1, source_target_pairs={{0,13},{1,12},{2,15},{3,14},{4,9},{5,8},{6,11},{7,10},{8,5},{9,4},... | collective-permute-start | bytes 393224 | tf_op jit(solution)/shard_map/ppermute | solution.py:652
  227.5 32.1 %collective-permute-start.26 = (f32[1,2,2,64,128]{4,3,2,1,0:T(8,128)S(1)}, f32[1,2,2,64,128]{4,3,2,1,0:T(8,128)S(1)}, u32[]{:S(2)}, u32[]{:S(2)}) collective-permute-start(f32[1,2,2,64,128]{4,3,2,1,0:T(8,128)S(1)} %bitcast.135), channel_id=1, source_target_pairs={{0,12},{1,13},{2,14},{3,15},{4,8},{5,9},{6,10},{7,11},{8,4},{9,5},... | collective-permute-start | bytes 393224 | tf_op jit(solution)/shard_map/ppermute | solution.py:652
  228.6 33.2 %collective-permute-start.25 = (f32[1,2,2,64,128]{4,3,2,1,0:T(8,128)S(1)}, f32[1,2,2,64,128]{4,3,2,1,0:T(8,128)S(1)}, u32[]{:S(2)}, u32[]{:S(2)}) collective-permute-start(f32[1,2,2,64,128]{4,3,2,1,0:T(8,128)S(1)} %bitcast.131), channel_id=1, source_target_pairs={{0,11},{1,10},{2,9},{3,8},{4,15},{5,14},{6,13},{7,12},{8,3},{9,2},... | collective-permute-start | bytes 393224 | tf_op jit(solution)/shard_map/ppermute | solution.py:652
  236.9 30.5 %collective-permute-start.24 = (f32[1,2,2,64,128]{4,3,2,1,0:T(8,128)S(1)}, f32[1,2,2,64,128]{4,3,2,1,0:T(8,128)S(1)}, u32[]{:S(2)}, u32[]{:S(2)}) collective-permute-start(f32[1,2,2,64,128]{4,3,2,1,0:T(8,128)S(1)} %bitcast.127), channel_id=1, source_target_pairs={{0,10},{1,11},{2,8},{3,9},{4,14},{5,15},{6,12},{7,13},{8,2},{9,3},... | collective-permute-start | bytes 393224 | tf_op jit(solution)/shard_map/ppermute | solution.py:652
  251.2 18.7 %collective-permute-start.23 = (f32[1,2,2,64,128]{4,3,2,1,0:T(8,128)S(1)}, f32[1,2,2,64,128]{4,3,2,1,0:T(8,128)S(1)}, u32[]{:S(2)}, u32[]{:S(2)}) collective-permute-start(f32[1,2,2,64,128]{4,3,2,1,0:T(8,128)S(1)} %bitcast.123), channel_id=1, source_target_pairs={{0,9},{1,8},{2,11},{3,10},{4,13},{5,12},{6,15},{7,14},{8,1},{9,0},... | collective-permute-start | bytes 393224 | tf_op jit(solution)/shard_map/ppermute | solution.py:652
  258.3 14.5 %collective-permute-start.22 = (f32[1,2,2,64,128]{4,3,2,1,0:T(8,128)S(1)}, f32[1,2,2,64,128]{4,3,2,1,0:T(8,128)S(1)}, u32[]{:S(2)}, u32[]{:S(2)}) collective-permute-start(f32[1,2,2,64,128]{4,3,2,1,0:T(8,128)S(1)} %bitcast.119), channel_id=1, source_target_pairs={{0,8},{1,9},{2,10},{3,11},{4,12},{5,13},{6,14},{7,15},{8,0},{9,1},... | collective-permute-start | bytes 393224 | tf_op jit(solution)/shard_map/ppermute | solution.py:652
  259.6 13.8 %collective-permute-start.21 = (f32[1,2,2,64,128]{4,3,2,1,0:T(8,128)S(1)}, f32[1,2,2,64,128]{4,3,2,1,0:T(8,128)S(1)}, u32[]{:S(2)}, u32[]{:S(2)}) collective-permute-start(f32[1,2,2,64,128]{4,3,2,1,0:T(8,128)S(1)} %bitcast.115), channel_id=1, source_target_pairs={{0,7},{1,6},{2,5},{3,4},{4,3},{5,2},{6,1},{7,0},{8,15},{9,14},{10,... | collective-permute-start | bytes 393224 | tf_op jit(solution)/shard_map/ppermute | solution.py:652
  261.8 13.2 %collective-permute-start.20 = (f32[1,2,2,64,128]{4,3,2,1,0:T(8,128)S(1)}, f32[1,2,2,64,128]{4,3,2,1,0:T(8,128)S(1)}, u32[]{:S(2)}, u32[]{:S(2)}) collective-permute-start(f32[1,2,2,64,128]{4,3,2,1,0:T(8,128)S(1)} %bitcast.111), channel_id=1, source_target_pairs={{0,6},{1,7},{2,4},{3,5},{4,2},{5,3},{6,0},{7,1},{8,14},{9,15},{10,... | collective-permute-start | bytes 393224 | tf_op jit(solution)/shard_map/ppermute | solution.py:652
  267.4 11.2 %collective-permute-start.19 = (f32[1,2,2,64,128]{4,3,2,1,0:T(8,128)S(1)}, f32[1,2,2,64,128]{4,3,2,1,0:T(8,128)S(1)}, u32[]{:S(2)}, u32[]{:S(2)}) collective-permute-start(f32[1,2,2,64,128]{4,3,2,1,0:T(8,128)S(1)} %bitcast.108), channel_id=1, source_target_pairs={{0,5},{1,4},{2,7},{3,6},{4,1},{5,0},{6,3},{7,2},{8,13},{9,12},{10,... | collective-permute-start | bytes 393224 | tf_op jit(solution)/shard_map/ppermute | solution.py:652
  377.8 192.5 %all-to-all-start.3 = ((f32[16,2,2,64,128]{4,3,2,1,0:T(8,128)}), f32[16,2,2,64,128]{4,3,2,1,0:T(8,128)}, u32[]{:S(2)}, u32[]{:S(2)}) async-start(f32[16,2,2,64,128]{4,3,2,1,0:T(8,128)} %bitcast.87), calls=%async_computation.3 | async-start | bytes 4194304 | tf_op jit(solution)/shard_map/all_to_all | solution.py:648
  408.0 39.4 %collective-permute-start.43 = (f32[1,2,2,64,128]{4,3,2,1,0:T(8,128)S(1)}, f32[1,2,2,64,128]{4,3,2,1,0:T(8,128)S(1)}, u32[]{:S(2)}, u32[]{:S(2)}) collective-permute-start(f32[1,2,2,64,128]{4,3,2,1,0:T(8,128)S(1)} %bitcast.148), channel_id=1, source_target_pairs={{0,14},{1,15},{2,12},{3,13},{4,10},{5,11},{6,8},{7,9},{8,6},{9,7},... | collective-permute-start | bytes 393224 | tf_op jit(solution)/shard_map/ppermute | solution.py:652
  410.1 40.9 %collective-permute-start.44 = (f32[1,2,2,64,128]{4,3,2,1,0:T(8,128)S(1)}, f32[1,2,2,64,128]{4,3,2,1,0:T(8,128)S(1)}, u32[]{:S(2)}, u32[]{:S(2)}) collective-permute-start(f32[1,2,2,64,128]{4,3,2,1,0:T(8,128)S(1)} %bitcast.144), channel_id=1, source_target_pairs={{0,15},{1,14},{2,13},{3,12},{4,11},{5,10},{6,9},{7,8},{8,7},{9,6},... | collective-permute-start | bytes 393224 | tf_op jit(solution)/shard_map/ppermute | solution.py:652
  410.9 47.5 %collective-permute-start.42 = (f32[1,2,2,64,128]{4,3,2,1,0:T(8,128)S(1)}, f32[1,2,2,64,128]{4,3,2,1,0:T(8,128)S(1)}, u32[]{:S(2)}, u32[]{:S(2)}) collective-permute-start(f32[1,2,2,64,128]{4,3,2,1,0:T(8,128)S(1)} %bitcast.140), channel_id=1, source_target_pairs={{0,13},{1,12},{2,15},{3,14},{4,9},{5,8},{6,11},{7,10},{8,5},{9,4},... | collective-permute-start | bytes 393224 | tf_op jit(solution)/shard_map/ppermute | solution.py:652
  411.9 48.5 %collective-permute-start.41 = (f32[1,2,2,64,128]{4,3,2,1,0:T(8,128)S(1)}, f32[1,2,2,64,128]{4,3,2,1,0:T(8,128)S(1)}, u32[]{:S(2)}, u32[]{:S(2)}) collective-permute-start(f32[1,2,2,64,128]{4,3,2,1,0:T(8,128)S(1)} %bitcast.136), channel_id=1, source_target_pairs={{0,12},{1,13},{2,14},{3,15},{4,8},{5,9},{6,10},{7,11},{8,4},{9,5},... | collective-permute-start | bytes 393224 | tf_op jit(solution)/shard_map/ppermute | solution.py:652
  412.1 52.0 %collective-permute-start.40 = (f32[1,2,2,64,128]{4,3,2,1,0:T(8,128)S(1)}, f32[1,2,2,64,128]{4,3,2,1,0:T(8,128)S(1)}, u32[]{:S(2)}, u32[]{:S(2)}) collective-permute-start(f32[1,2,2,64,128]{4,3,2,1,0:T(8,128)S(1)} %bitcast.132), channel_id=1, source_target_pairs={{0,11},{1,10},{2,9},{3,8},{4,15},{5,14},{6,13},{7,12},{8,3},{9,2},... | collective-permute-start | bytes 393224 | tf_op jit(solution)/shard_map/ppermute | solution.py:652
  447.3 21.7 %collective-permute-start.39 = (f32[1,2,2,64,128]{4,3,2,1,0:T(8,128)S(1)}, f32[1,2,2,64,128]{4,3,2,1,0:T(8,128)S(1)}, u32[]{:S(2)}, u32[]{:S(2)}) collective-permute-start(f32[1,2,2,64,128]{4,3,2,1,0:T(8,128)S(1)} %bitcast.128), channel_id=1, source_target_pairs={{0,10},{1,11},{2,8},{3,9},{4,14},{5,15},{6,12},{7,13},{8,2},{9,3},... | collective-permute-start | bytes 393224 | tf_op jit(solution)/shard_map/ppermute | solution.py:652
  451.0 21.5 %collective-permute-start.38 = (f32[1,2,2,64,128]{4,3,2,1,0:T(8,128)S(1)}, f32[1,2,2,64,128]{4,3,2,1,0:T(8,128)S(1)}, u32[]{:S(2)}, u32[]{:S(2)}) collective-permute-start(f32[1,2,2,64,128]{4,3,2,1,0:T(8,128)S(1)} %bitcast.124), channel_id=1, source_target_pairs={{0,9},{1,8},{2,11},{3,10},{4,13},{5,12},{6,15},{7,14},{8,1},{9,0},... | collective-permute-start | bytes 393224 | tf_op jit(solution)/shard_map/ppermute | solution.py:652
  458.5 15.3 %collective-permute-start.37 = (f32[1,2,2,64,128]{4,3,2,1,0:T(8,128)S(1)}, f32[1,2,2,64,128]{4,3,2,1,0:T(8,128)S(1)}, u32[]{:S(2)}, u32[]{:S(2)}) collective-permute-start(f32[1,2,2,64,128]{4,3,2,1,0:T(8,128)S(1)} %bitcast.120), channel_id=1, source_target_pairs={{0,8},{1,9},{2,10},{3,11},{4,12},{5,13},{6,14},{7,15},{8,0},{9,1},... | collective-permute-start | bytes 393224 | tf_op jit(solution)/shard_map/ppermute | solution.py:652
  460.4 14.3 %collective-permute-start.36 = (f32[1,2,2,64,128]{4,3,2,1,0:T(8,128)S(1)}, f32[1,2,2,64,128]{4,3,2,1,0:T(8,128)S(1)}, u32[]{:S(2)}, u32[]{:S(2)}) collective-permute-start(f32[1,2,2,64,128]{4,3,2,1,0:T(8,128)S(1)} %bitcast.116), channel_id=1, source_target_pairs={{0,7},{1,6},{2,5},{3,4},{4,3},{5,2},{6,1},{7,0},{8,15},{9,14},{10,... | collective-permute-start | bytes 393224 | tf_op jit(solution)/shard_map/ppermute | solution.py:652
  464.1 12.8 %collective-permute-start.35 = (f32[1,2,2,64,128]{4,3,2,1,0:T(8,128)S(1)}, f32[1,2,2,64,128]{4,3,2,1,0:T(8,128)S(1)}, u32[]{:S(2)}, u32[]{:S(2)}) collective-permute-start(f32[1,2,2,64,128]{4,3,2,1,0:T(8,128)S(1)} %bitcast.112), channel_id=1, source_target_pairs={{0,6},{1,7},{2,4},{3,5},{4,2},{5,3},{6,0},{7,1},{8,14},{9,15},{10,... | collective-permute-start | bytes 393224 | tf_op jit(solution)/shard_map/ppermute | solution.py:652
  500.9 12.2 %collective-permute-start.58 = (f32[1,2,2,64,128]{4,3,2,1,0:T(8,128)S(1)}, f32[1,2,2,64,128]{4,3,2,1,0:T(8,128)S(1)}, u32[]{:S(2)}, u32[]{:S(2)}) collective-permute-start(f32[1,2,2,64,128]{4,3,2,1,0:T(8,128)S(1)} %bitcast.149), channel_id=1, source_target_pairs={{0,14},{1,15},{2,12},{3,13},{4,10},{5,11},{6,8},{7,9},{8,6},{9,7},... | collective-permute-start | bytes 393224 | tf_op jit(solution)/shard_map/ppermute | solution.py:652
  502.0 25.5 %collective-permute-start.59 = (f32[1,2,2,64,128]{4,3,2,1,0:T(8,128)S(1)}, f32[1,2,2,64,128]{4,3,2,1,0:T(8,128)S(1)}, u32[]{:S(2)}, u32[]{:S(2)}) collective-permute-start(f32[1,2,2,64,128]{4,3,2,1,0:T(8,128)S(1)} %bitcast.145), channel_id=1, source_target_pairs={{0,15},{1,14},{2,13},{3,12},{4,11},{5,10},{6,9},{7,8},{8,7},{9,6},... | collective-permute-start | bytes 393224 | tf_op jit(solution)/shard_map/ppermute | solution.py:652
  503.8 30.9 %collective-permute-start.57 = (f32[1,2,2,64,128]{4,3,2,1,0:T(8,128)S(1)}, f32[1,2,2,64,128]{4,3,2,1,0:T(8,128)S(1)}, u32[]{:S(2)}, u32[]{:S(2)}) collective-permute-start(f32[1,2,2,64,128]{4,3,2,1,0:T(8,128)S(1)} %bitcast.141), channel_id=1, source_target_pairs={{0,13},{1,12},{2,15},{3,14},{4,9},{5,8},{6,11},{7,10},{8,5},{9,4},... | collective-permute-start | bytes 393224 | tf_op jit(solution)/shard_map/ppermute | solution.py:652
  503.9 32.1 %collective-permute-start.56 = (f32[1,2,2,64,128]{4,3,2,1,0:T(8,128)S(1)}, f32[1,2,2,64,128]{4,3,2,1,0:T(8,128)S(1)}, u32[]{:S(2)}, u32[]{:S(2)}) collective-permute-start(f32[1,2,2,64,128]{4,3,2,1,0:T(8,128)S(1)} %bitcast.137), channel_id=1, source_target_pairs={{0,12},{1,13},{2,14},{3,15},{4,8},{5,9},{6,10},{7,11},{8,4},{9,5},... | collective-permute-start | bytes 393224 | tf_op jit(solution)/shard_map/ppermute | solution.py:652
  505.0 33.0 %collective-permute-start.55 = (f32[1,2,2,64,128]{4,3,2,1,0:T(8,128)S(1)}, f32[1,2,2,64,128]{4,3,2,1,0:T(8,128)S(1)}, u32[]{:S(2)}, u32[]{:S(2)}) collective-permute-start(f32[1,2,2,64,128]{4,3,2,1,0:T(8,128)S(1)} %bitcast.133), channel_id=1, source_target_pairs={{0,11},{1,10},{2,9},{3,8},{4,15},{5,14},{6,13},{7,12},{8,3},{9,2},... | collective-permute-start | bytes 393224 | tf_op jit(solution)/shard_map/ppermute | solution.py:652
  513.1 30.7 %collective-permute-start.54 = (f32[1,2,2,64,128]{4,3,2,1,0:T(8,128)S(1)}, f32[1,2,2,64,128]{4,3,2,1,0:T(8,128)S(1)}, u32[]{:S(2)}, u32[]{:S(2)}) collective-permute-start(f32[1,2,2,64,128]{4,3,2,1,0:T(8,128)S(1)} %bitcast.129), channel_id=1, source_target_pairs={{0,10},{1,11},{2,8},{3,9},{4,14},{5,15},{6,12},{7,13},{8,2},{9,3},... | collective-permute-start | bytes 393224 | tf_op jit(solution)/shard_map/ppermute | solution.py:652
  527.5 18.7 %collective-permute-start.53 = (f32[1,2,2,64,128]{4,3,2,1,0:T(8,128)S(1)}, f32[1,2,2,64,128]{4,3,2,1,0:T(8,128)S(1)}, u32[]{:S(2)}, u32[]{:S(2)}) collective-permute-start(f32[1,2,2,64,128]{4,3,2,1,0:T(8,128)S(1)} %bitcast.125), channel_id=1, source_target_pairs={{0,9},{1,8},{2,11},{3,10},{4,13},{5,12},{6,15},{7,14},{8,1},{9,0},... | collective-permute-start | bytes 393224 | tf_op jit(solution)/shard_map/ppermute | solution.py:652
  534.7 13.8 %collective-permute-start.52 = (f32[1,2,2,64,128]{4,3,2,1,0:T(8,128)S(1)}, f32[1,2,2,64,128]{4,3,2,1,0:T(8,128)S(1)}, u32[]{:S(2)}, u32[]{:S(2)}) collective-permute-start(f32[1,2,2,64,128]{4,3,2,1,0:T(8,128)S(1)} %bitcast.121), channel_id=1, source_target_pairs={{0,8},{1,9},{2,10},{3,11},{4,12},{5,13},{6,14},{7,15},{8,0},{9,1},... | collective-permute-start | bytes 393224 | tf_op jit(solution)/shard_map/ppermute | solution.py:652
  536.0 12.6 %collective-permute-start.51 = (f32[1,2,2,64,128]{4,3,2,1,0:T(8,128)S(1)}, f32[1,2,2,64,128]{4,3,2,1,0:T(8,128)S(1)}, u32[]{:S(2)}, u32[]{:S(2)}) collective-permute-start(f32[1,2,2,64,128]{4,3,2,1,0:T(8,128)S(1)} %bitcast.117), channel_id=1, source_target_pairs={{0,7},{1,6},{2,5},{3,4},{4,3},{5,2},{6,1},{7,0},{8,15},{9,14},{10,... | collective-permute-start | bytes 393224 | tf_op jit(solution)/shard_map/ppermute | solution.py:652
  538.1 13.3 %collective-permute-start.50 = (f32[1,2,2,64,128]{4,3,2,1,0:T(8,128)S(1)}, f32[1,2,2,64,128]{4,3,2,1,0:T(8,128)S(1)}, u32[]{:S(2)}, u32[]{:S(2)}) collective-permute-start(f32[1,2,2,64,128]{4,3,2,1,0:T(8,128)S(1)} %bitcast.113), channel_id=1, source_target_pairs={{0,6},{1,7},{2,4},{3,5},{4,2},{5,3},{6,0},{7,1},{8,14},{9,15},{10,... | collective-permute-start | bytes 393224 | tf_op jit(solution)/shard_map/ppermute | solution.py:652
  543.8 15.8 %collective-permute-start.49 = (f32[1,2,2,64,128]{4,3,2,1,0:T(8,128)}, f32[1,2,2,64,128]{4,3,2,1,0:T(8,128)S(1)}, u32[]{:S(2)}, u32[]{:S(2)}) collective-permute-start(f32[1,2,2,64,128]{4,3,2,1,0:T(8,128)} %bitcast.63), channel_id=1, source_target_pairs={{0,5},{1,4},{2,7},{3,6},{4,1},{5,0},{6,3},{7,2},{8,13},{9,12},{10,... | collective-permute-start | bytes 393224 | tf_op jit(solution)/shard_map/ppermute | solution.py:652
  546.3 13.4 %collective-permute-start.48 = (f32[1,2,2,64,128]{4,3,2,1,0:T(8,128)}, f32[1,2,2,64,128]{4,3,2,1,0:T(8,128)S(1)}, u32[]{:S(2)}, u32[]{:S(2)}) collective-permute-start(f32[1,2,2,64,128]{4,3,2,1,0:T(8,128)} %bitcast.62), channel_id=1, source_target_pairs={{0,4},{1,5},{2,6},{3,7},{4,0},{5,1},{6,2},{7,3},{8,12},{9,13},{10,... | collective-permute-start | bytes 393224 | tf_op jit(solution)/shard_map/ppermute | solution.py:652
  548.5 11.1 %collective-permute-start.47 = (f32[1,2,2,64,128]{4,3,2,1,0:T(8,128)}, f32[1,2,2,64,128]{4,3,2,1,0:T(8,128)S(1)}, u32[]{:S(2)}, u32[]{:S(2)}) collective-permute-start(f32[1,2,2,64,128]{4,3,2,1,0:T(8,128)} %bitcast.61), channel_id=1, source_target_pairs={{0,3},{1,2},{2,1},{3,0},{4,7},{5,6},{6,5},{7,4},{8,11},{9,10},{10,... | collective-permute-start | bytes 393224 | tf_op jit(solution)/shard_map/ppermute | solution.py:652
  548.5 11.1 %collective-permute-start.46 = (f32[1,2,2,64,128]{4,3,2,1,0:T(8,128)}, f32[1,2,2,64,128]{4,3,2,1,0:T(8,128)S(1)}, u32[]{:S(2)}, u32[]{:S(2)}) collective-permute-start(f32[1,2,2,64,128]{4,3,2,1,0:T(8,128)} %bitcast.60), channel_id=1, source_target_pairs={{0,2},{1,3},{2,0},{3,1},{4,6},{5,7},{6,4},{7,5},{8,10},{9,11},{10,... | collective-permute-start | bytes 393224 | tf_op jit(solution)/shard_map/ppermute | solution.py:652
  (84 other events, 683.2 us)
